TPU v7x, 256 devices: a whole 4x4x8 slice. The times are simulated.
256 devices in a mesh: dom: 128 (over z, y, x), col: 2 (over core).
Axes of the slice: x: 4, y: 4, z: 8, core: 2. Of those that a mesh axis runs over, the one named last changes fastest.
Arguments:
- seed_data: bfloat16 [524288, 256], P('dom', 'col'), may hold values from -40 to 40
- dataset_order: int32 [128, 4096], P('dom'), may hold values from 0 to 4095, each once within a row
- affinity: bfloat16 [4096, 16, 128, 128], P('dom'), may hold values from 9.952637e-21 to 1
- neighbour_tiles: int32 [4096, 16], P('dom'), may hold values from 0 to 4095, as said below
- clamp_mask: int32 [524288], P('dom'), may hold values 0 or 1
Outputs:
- labels: bfloat16 [524288, 256], P('dom', 'col')
Inputs may be any that keep to these rules, and one draw needn't show every extreme that they name: `neighbour_tiles`: slot 0 of row tile t is t itself. Every id names a tile of the row tile's own partition (id // 32) or of the partition just below or above it; partition 0 names none below and the last partition none above. Over all row tiles of one partition at most 4 distinct tiles of each neighbouring partition are named, and partition 0 names exactly 4 tiles of partition 1.
All inputs are finite; a program needn't handle non-finite values. No bound on the sum of `clamp_mask` on one device may be relied on, other than what follows from the above.
Results may differ from a plain program's by a relative error of at most 0.001.
Values may be sent and summed in bfloat16 or wider, within the bound.
No kernel may reach another device: no remote copies, remote signals or barrier semaphores. Data moves between devices by JAX's collectives and lax.ppermute only.
A program may use at most 128 MiB of HBM per device.

v0:
```python
import jax
import jax.numpy as jnp
from jax import lax
from jax.sharding import PartitionSpec as P

ITERS = 3


carry_weight = 0.9
norm_eps = 1e-05


def shifted(block, axis, distance):
    devices = range(lax.axis_size(axis))
    route = [(i - distance, i) for i in devices if i - distance in devices]
    return lax.ppermute(block, axis, route)


def per_device(seed_data, dataset_order, affinity, neighbour_tiles, clamp_mask):
    part_count = lax.axis_size("dom")
    my_part = lax.axis_index("dom")
    cell_count = seed_data.shape[0]
    slab_width = seed_data.shape[1]
    per_source = cell_count // part_count
    tile_count = affinity.shape[0]
    tile_rows = affinity.shape[2]
    pieces = seed_data.reshape(part_count, per_source, slab_width)
    arrived = lax.all_to_all(pieces, "dom", split_axis=0, concat_axis=0, tiled=True).reshape(
        cell_count, slab_width
    )
    clamped_label_rows = arrived[dataset_order[0]]
    seed_float = clamped_label_rows.astype(jnp.float32)
    degree = jnp.sum(affinity, axis=(1, 3), dtype=jnp.float32).reshape(cell_count, 1)
    owners = neighbour_tiles // tile_count
    within = neighbour_tiles % tile_count
    offset = owners - my_part
    label_total = slab_width * lax.axis_size("col")
    pool_index = (offset + 1) * tile_count + within
    labels = clamped_label_rows
    for iteration in range(ITERS):
        own_tiles = labels.reshape(tile_count, tile_rows, slab_width)
        from_left = shifted(labels, "dom", 1)
        from_right = shifted(labels, "dom", -1)
        tile_pool = jnp.concatenate(
            [
                from_left.reshape(tile_count, tile_rows, slab_width),
                own_tiles,
                from_right.reshape(tile_count, tile_rows, slab_width),
            ],
            axis=0,
        )
        gathered_rows = tile_pool[pool_index]
        diffused_labels = jnp.einsum(
            "xzeh,xzhj->xej", affinity, gathered_rows, preferred_element_type=jnp.float32
        )
        diffused_labels = diffused_labels.reshape(cell_count, slab_width)
        mixed = carry_weight * diffused_labels / degree + (1.0 - carry_weight) * seed_float
        squared_entries = lax.psum(jnp.sum(mixed * mixed, axis=1), "col")
        row_scale = jnp.sqrt(squared_entries / label_total + norm_eps)
        labels = jnp.where(clamp_mask[:, None] == 1, seed_float, mixed / row_scale[:, None]).astype(
            jnp.bfloat16
        )
    return labels


def solution(mesh):
    return jax.shard_map(
        per_device,
        mesh=mesh,
        in_specs=(
            P("dom", "col"),
            P("dom", None),
            P("dom", None, None, None),
            P("dom", None),
            P("dom"),
        ),
        out_specs=P("dom", "col"),
        check_vma=False,
    )
```

profile of v0, /device:TPU:33, one launch (start us, length us, event | category | flops | bytes accessed | tf_op | source)
XLA Modules:
  0.0 270.3 jit_solution(1301881378200343303)
XLA Ops:
  0.0 14.6 %all-to-all-start = ((bf16[128,32,128]{2,1,0:T(8,128)(2,1)}), bf16[128,32,128]{2,1,0:T(8,128)(2,1)S(1)}, u32[]{:S(2)}, u32[]{:S(2)}) async-start(bf16[128,32,128]{2,1,0:T(8,128)(2,1)} %bitcast.88), calls=%async_computation | async-start | bytes 2097152 | tf_op jit(solution)/shard_map/all_to_all | solution.py:28
  14.9 29.0 %all-to-all-done = bf16[128,32,128]{2,1,0:T(8,128)(2,1)S(1)} async-done(((bf16[128,32,128]{2,1,0:T(8,128)(2,1)}), bf16[128,32,128]{2,1,0:T(8,128)(2,1)S(1)}, u32[]{:S(2)}, u32[]{:S(2)}) %all-to-all-start) | async-done | bytes 1048608 | tf_op jit(solution)/shard_map/all_to_all | solution.py:28
  43.8 12.1 %gather_fusion = bf16[4096,128]{1,0:T(8,128)(2,1)S(1)} fusion(bf16[4096,128]{1,0:T(8,128)(2,1)S(1)} %bitcast.80, s32[4096]{0:T(1024)S(1)} %broadcast_clamp_fusion), kind=kCustom, calls=%fused_computation | custom fusion | bytes 2113536 | tf_op jit(solution)/shard_map/gather | solution.py:31
  56.0 2.4 collective-permute-start
  58.4 7.1 %collective-permute-start.1 = (bf16[4096,128]{1,0:T(8,128)(2,1)S(1)}, bf16[4096,128]{1,0:T(8,128)(2,1)S(1)}, u32[]{:S(2)}, u32[]{:S(2)}) collective-permute-start(bf16[4096,128]{1,0:T(8,128)(2,1)S(1)} %gather_fusion), channel_id=1, source_target_pairs={{2,0},{4,2},{6,4},{8,6},{10,8},{12,10},{14,12},{16,14},{18,16},{20... | collective-permute-start | bytes 3145736 | tf_op jit(solution)/shard_map/ppermute | solution.py:16
  65.5 6.8 %convert_reduce_fusion = f32[32,128]{1,0:T(8,128)S(1)} fusion(bf16[32,16,128,128]{3,2,1,0:T(8,128)(2,1)} %param.7), kind=kLoop, calls=%fused_computation.4 | loop fusion | flops 16773120 | bytes 16793600 | tf_op jit(solution)/shard_map/reduce_sum | solution.py:33
  72.4 11.1 %collective-permute-done = bf16[4096,128]{1,0:T(8,128)(2,1)S(1)} collective-permute-done((bf16[4096,128]{1,0:T(8,128)(2,1)S(1)}, bf16[4096,128]{1,0:T(8,128)(2,1)S(1)}, u32[]{:S(2)}, u32[]{:S(2)}) %collective-permute-start) | collective-permute-done | bytes 1048608 | tf_op jit(solution)/shard_map/ppermute | solution.py:16
  85.8 13.9 %gather_fusion.1 = bf16[512,128,128]{2,1,0:T(8,128)(2,1)} fusion(bf16[96,128,128]{2,1,0:T(8,128)(2,1)S(1)} %pad_maximum_fusion, s32[1024]{0:T(1024)S(1)} %pad_clamp_fusion), kind=kCustom, calls=%fused_computation.1 | custom fusion | bytes 33556480 | tf_op jit(solution)/shard_map/gather | solution.py:52
  99.7 15.3 %multiply_reduce_fusion.1 = (f32[32,128]{1,0:T(8,128)S(1)}, f32[32,128,128]{1,2,0:T(8,128)S(1)}) fusion(bf16[32,128,128]{2,1,0:T(8,128)(2,1)} %bitcast.82, f32[32,128]{1,0:T(8,128)S(1)} %convert_reduce_fusion, bf16[32,16,128,128]{3,2,1,0:T(8,128)(2,1)} %param.7, bf16[32,16,128,128]{3,2,1,0:T(8,128)(2,1)} %bitcast.86), kind=kOutput, calls=%fused_computation.35 | convolution fusion | flops 2151149568 | bytes 36732928 | tf_op jit(solution)/shard_map/xzeh,xzhj->xej/dot_general | solution.py:53
  115.0 7.7 %psum.21 = f32[4096]{0:T(1024)S(1)} all-reduce(f32[4096]{0:T(1024)S(1)} %bitcast.99), channel_id=1, replica_groups=mesh['dom'=128,'col'=2] {'col'}, use_global_device_ids=true, to_apply=%region_2.3 | all-reduce | flops 4096 | bytes 32768 | tf_op jit(solution)/shard_map/psum | solution.py:58
  122.7 2.1 fusion.13
  124.8 8.3 %collective-permute-start.3 = (bf16[4096,128]{1,0:T(8,128)(2,1)S(1)}, bf16[4096,128]{1,0:T(8,128)(2,1)S(1)}, u32[]{:S(2)}, u32[]{:S(2)}) collective-permute-start(bf16[4096,128]{1,0:T(8,128)(2,1)S(1)} %fusion.13), channel_id=1, source_target_pairs={{2,0},{4,2},{6,4},{8,6},{10,8},{12,10},{14,12},{16,14},{18,16},{20... | collective-permute-start | bytes 3145736 | tf_op jit(solution)/shard_map/ppermute | solution.py:16
  137.2 18.3 %collective-permute-done.3 = bf16[4096,128]{1,0:T(8,128)(2,1)S(1)} collective-permute-done((bf16[4096,128]{1,0:T(8,128)(2,1)S(1)}, bf16[4096,128]{1,0:T(8,128)(2,1)S(1)}, u32[]{:S(2)}, u32[]{:S(2)}) %collective-permute-start.3) | collective-permute-done | bytes 1048608 | tf_op jit(solution)/shard_map/ppermute | solution.py:16
  155.4 8.1 %collective-permute-done.2 = bf16[4096,128]{1,0:T(8,128)(2,1)S(1)} collective-permute-done((bf16[4096,128]{1,0:T(8,128)(2,1)S(1)}, bf16[4096,128]{1,0:T(8,128)(2,1)S(1)}, u32[]{:S(2)}, u32[]{:S(2)}) %collective-permute-start.2) | collective-permute-done | bytes 1048608 | tf_op jit(solution)/shard_map/ppermute | solution.py:16
  163.9 13.9 %gather_fusion.2 = bf16[512,128,128]{2,1,0:T(8,128)(2,1)} fusion(bf16[96,128,128]{2,1,0:T(8,128)(2,1)S(1)} %pad_maximum_fusion.1, s32[1024]{0:T(1024)S(1)} %pad_clamp_fusion), kind=kCustom, calls=%fused_computation.2 | custom fusion | bytes 33556480 | tf_op jit(solution)/shard_map/gather | solution.py:52
  177.8 15.3 %multiply_reduce_fusion = (f32[32,128]{1,0:T(8,128)S(1)}, f32[32,128,128]{1,2,0:T(8,128)S(1)}) fusion(bf16[32,128,128]{2,1,0:T(8,128)(2,1)} %bitcast.83, f32[32,128]{1,0:T(8,128)S(1)} %convert_reduce_fusion, bf16[32,16,128,128]{3,2,1,0:T(8,128)(2,1)} %param.7, bf16[32,16,128,128]{3,2,1,0:T(8,128)(2,1)} %bitcast.87), kind=kOutput, calls=%fused_computation.34 | convolution fusion | flops 2151149568 | bytes 36732928 | tf_op jit(solution)/shard_map/xzeh,xzhj->xej/dot_general | solution.py:53
  193.1 4.5 %psum.22 = f32[4096]{0:T(1024)S(1)} all-reduce(f32[4096]{0:T(1024)S(1)} %bitcast.100), channel_id=1, replica_groups=mesh['dom'=128,'col'=2] {'col'}, use_global_device_ids=true, to_apply=%region_4.5 | all-reduce | flops 4096 | bytes 32768 | tf_op jit(solution)/shard_map/psum | solution.py:58
  201.6 3.6 %collective-permute-start.4 = (bf16[4096,128]{1,0:T(8,128)(2,1)S(1)}, bf16[4096,128]{1,0:T(8,128)(2,1)S(1)}, u32[]{:S(2)}, u32[]{:S(2)}) collective-permute-start(bf16[4096,128]{1,0:T(8,128)(2,1)S(1)} %fusion.14), channel_id=1, source_target_pairs={{0,2},{2,4},{4,6},{6,8},{8,10},{10,12},{12,14},{14,16},{16,18},{18... | collective-permute-start | bytes 3145736 | tf_op jit(solution)/shard_map/ppermute | solution.py:16
  207.2 19.0 %collective-permute-done.5 = bf16[4096,128]{1,0:T(8,128)(2,1)S(1)} collective-permute-done((bf16[4096,128]{1,0:T(8,128)(2,1)S(1)}, bf16[4096,128]{1,0:T(8,128)(2,1)S(1)}, u32[]{:S(2)}, u32[]{:S(2)}) %collective-permute-start.5) | collective-permute-done | bytes 1048608 | tf_op jit(solution)/shard_map/ppermute | solution.py:16
  226.1 6.1 %collective-permute-done.4 = bf16[4096,128]{1,0:T(8,128)(2,1)S(1)} collective-permute-done((bf16[4096,128]{1,0:T(8,128)(2,1)S(1)}, bf16[4096,128]{1,0:T(8,128)(2,1)S(1)}, u32[]{:S(2)}, u32[]{:S(2)}) %collective-permute-start.4) | collective-permute-done | bytes 1048608 | tf_op jit(solution)/shard_map/ppermute | solution.py:16
  232.7 13.9 %gather_fusion.3 = bf16[512,128,128]{2,1,0:T(8,128)(2,1)} fusion(bf16[96,128,128]{2,1,0:T(8,128)(2,1)S(1)} %pad_maximum_fusion.2, s32[1024]{0:T(1024)S(1)} %pad_clamp_fusion), kind=kCustom, calls=%fused_computation.3 | custom fusion | bytes 33556480 | tf_op jit(solution)/shard_map/gather | solution.py:52
  246.5 15.3 %fusion.10 = (f32[32,128]{1,0:T(8,128)S(1)}, f32[32,128,128]{1,2,0:T(8,128)S(1)}) fusion(bf16[32,128,128]{2,1,0:T(8,128)(2,1)} %bitcast.84, f32[32,128]{1,0:T(8,128)S(1)} %convert_reduce_fusion, bf16[32,16,128,128]{3,2,1,0:T(8,128)(2,1)} %param.7, bf16[32,16,128,128]{3,2,1,0:T(8,128)(2,1)} %bitcast.85), kind=kOutput, calls=%fused_computation.25 | convolution fusion | flops 2151149568 | bytes 36732928 | tf_op jit(solution)/shard_map/xzeh,xzhj->xej/dot_general | solution.py:53
  261.9 4.2 %psum.23 = f32[4096]{0:T(1024)S(1)} all-reduce(f32[4096]{0:T(1024)S(1)} %bitcast.101), channel_id=1, replica_groups=mesh['dom'=128,'col'=2] {'col'}, use_global_device_ids=true, to_apply=%region_6.7 | all-reduce | flops 4096 | bytes 32768 | tf_op jit(solution)/shard_map/psum | solution.py:58
  266.1 4.2 %fusion.15 = bf16[4096,128]{1,0:T(8,128)(2,1)} fusion(f32[32,128,128]{1,2,0:T(8,128)S(1)} %get-tuple-element.14, bf16[4096,128]{1,0:T(8,128)(2,1)S(1)} %copy-done.3, f32[4096]{0:T(1024)S(1)} %add_sqrt_fusion, f32[4096]{0:T(1024)S(1)} %bitcast.97, pred[4096]{0:T(1024)(128)(4,1)S(1)} %broadcast_compare_fusion), kind=kLoop, calls=%fused_computation.38 | loop fusion | flops 3670016 | bytes 4231168 | tf_op jit(solution)/shard_map/convert_element_type | solution.py:60
  (34 shorter events, 13.4 us)
Async XLA Ops:
  0.0 14.6 %copy-start.6 = (s32[32,16]{0,1:T(8,128)S(1)}, s32[32,16]{0,1:T(8,128)}, u32[]{:S(2)}) copy-start(s32[32,16]{0,1:T(8,128)} %param.8) | copy-start | bytes 6148
  0.0 14.8 %copy-start.4 = (s32[4096]{0:T(1024)S(1)}, s32[4096]{0:T(1024)}, u32[]{:S(2)}) copy-start(s32[4096]{0:T(1024)} %param.9) | copy-start | bytes 49156
  0.0 14.8 %copy-start.5 = (s32[1,4096]{1,0:T(1,128)S(1)}, s32[1,4096]{1,0:T(1,128)}, u32[]{:S(2)}) copy-start(s32[1,4096]{1,0:T(1,128)} %param.6) | copy-start | bytes 49156
  0.0 43.8 %all-to-all-start = ((bf16[128,32,128]{2,1,0:T(8,128)(2,1)}), bf16[128,32,128]{2,1,0:T(8,128)(2,1)S(1)}, u32[]{:S(2)}, u32[]{:S(2)}) async-start(bf16[128,32,128]{2,1,0:T(8,128)(2,1)} %bitcast.88), calls=%async_computation | async-start | bytes 2097152 | tf_op jit(solution)/shard_map/all_to_all | solution.py:28
  56.0 16.4 %copy-start = (bf16[4096,128]{1,0:T(8,128)(2,1)}, bf16[4096,128]{1,0:T(8,128)(2,1)S(1)}, u32[]{:S(2)}) copy-start(bf16[4096,128]{1,0:T(8,128)(2,1)S(1)} %gather_fusion) | copy-start | bytes 3145732
  56.0 27.5 %collective-permute-start = (bf16[4096,128]{1,0:T(8,128)(2,1)S(1)}, bf16[4096,128]{1,0:T(8,128)(2,1)S(1)}, u32[]{:S(2)}, u32[]{:S(2)}) collective-permute-start(bf16[4096,128]{1,0:T(8,128)(2,1)S(1)} %gather_fusion), channel_id=1, source_target_pairs={{0,2},{2,4},{4,6},{6,8},{8,10},{10,12},{12,14},{14,16},{16,18},{18... | collective-permute-start | bytes 3145736 | tf_op jit(solution)/shard_map/ppermute | solution.py:16
  58.4 26.0 %collective-permute-start.1 = (bf16[4096,128]{1,0:T(8,128)(2,1)S(1)}, bf16[4096,128]{1,0:T(8,128)(2,1)S(1)}, u32[]{:S(2)}, u32[]{:S(2)}) collective-permute-start(bf16[4096,128]{1,0:T(8,128)(2,1)S(1)} %gather_fusion), channel_id=1, source_target_pairs={{2,0},{4,2},{6,4},{8,6},{10,8},{12,10},{14,12},{16,14},{18,16},{20... | collective-permute-start | bytes 3145736 | tf_op jit(solution)/shard_map/ppermute | solution.py:16
  99.7 23.0 %copy-start.1 = (bf16[4096,128]{1,0:T(8,128)(2,1)S(1)}, bf16[4096,128]{1,0:T(8,128)(2,1)}, u32[]{:S(2)}) copy-start(bf16[4096,128]{1,0:T(8,128)(2,1)} %copy-done) | copy-start | bytes 3145732
  124.8 30.7 %collective-permute-start.3 = (bf16[4096,128]{1,0:T(8,128)(2,1)S(1)}, bf16[4096,128]{1,0:T(8,128)(2,1)S(1)}, u32[]{:S(2)}, u32[]{:S(2)}) collective-permute-start(bf16[4096,128]{1,0:T(8,128)(2,1)S(1)} %fusion.13), channel_id=1, source_target_pairs={{2,0},{4,2},{6,4},{8,6},{10,8},{12,10},{14,12},{16,14},{18,16},{20... | collective-permute-start | bytes 3145736 | tf_op jit(solution)/shard_map/ppermute | solution.py:16
  133.1 30.4 %collective-permute-start.2 = (bf16[4096,128]{1,0:T(8,128)(2,1)S(1)}, bf16[4096,128]{1,0:T(8,128)(2,1)S(1)}, u32[]{:S(2)}, u32[]{:S(2)}) collective-permute-start(bf16[4096,128]{1,0:T(8,128)(2,1)S(1)} %fusion.13), channel_id=1, source_target_pairs={{0,2},{2,4},{4,6},{6,8},{8,10},{10,12},{12,14},{14,16},{16,18},{18... | collective-permute-start | bytes 3145736 | tf_op jit(solution)/shard_map/ppermute | solution.py:16
  177.8 19.8 %copy-start.2 = (bf16[4096,128]{1,0:T(8,128)(2,1)S(1)}, bf16[4096,128]{1,0:T(8,128)(2,1)}, u32[]{:S(2)}) copy-start(bf16[4096,128]{1,0:T(8,128)(2,1)} %copy-done) | copy-start | bytes 3145732
  199.7 26.4 %collective-permute-start.5 = (bf16[4096,128]{1,0:T(8,128)(2,1)S(1)}, bf16[4096,128]{1,0:T(8,128)(2,1)S(1)}, u32[]{:S(2)}, u32[]{:S(2)}) collective-permute-start(bf16[4096,128]{1,0:T(8,128)(2,1)S(1)} %fusion.14), channel_id=1, source_target_pairs={{2,0},{4,2},{6,4},{8,6},{10,8},{12,10},{14,12},{16,14},{18,16},{20... | collective-permute-start | bytes 3145736 | tf_op jit(solution)/shard_map/ppermute | solution.py:16
  201.6 30.7 %collective-permute-start.4 = (bf16[4096,128]{1,0:T(8,128)(2,1)S(1)}, bf16[4096,128]{1,0:T(8,128)(2,1)S(1)}, u32[]{:S(2)}, u32[]{:S(2)}) collective-permute-start(bf16[4096,128]{1,0:T(8,128)(2,1)S(1)} %fusion.14), channel_id=1, source_target_pairs={{0,2},{2,4},{4,6},{6,8},{8,10},{10,12},{12,14},{14,16},{16,18},{18... | collective-permute-start | bytes 3145736 | tf_op jit(solution)/shard_map/ppermute | solution.py:16
  246.5 19.5 %copy-start.3 = (bf16[4096,128]{1,0:T(8,128)(2,1)S(1)}, bf16[4096,128]{1,0:T(8,128)(2,1)}, u32[]{:S(2)}) copy-start(bf16[4096,128]{1,0:T(8,128)(2,1)} %copy-done) | copy-start | bytes 3145732
where the time goes:
time: 271 us; the launch traced here: 270 us
  waiting for transfers between devices  92.4 us (34%)
  local copies, waits for them, and re-layouts  54 us (20%)
  matrix products  45.9 us (17%)
  starting transfers between devices  40 us (15%)
  other arithmetic  21.4 us (8%)
  blocking collectives  16.4 us (6%)
    ppermute x6, waiting for transfers between devices, shifted(): return lax.ppermute(block, axis, route)  63.4 us
    dot_general x3, matrix products, per_device(): jnp.einsum('xzeh,xzhj->xej', affinity, gathered_rows, preferred_element_t...  45.9 us
    gather x3, local copies, waits for them, and re-layouts, per_device(): gathered_rows = tile_pool[pool_index]  41.7 us
    all_to_all x1, waiting for transfers between devices, per_device(): lax.all_to_all(pieces, 'dom', split_axis=0, concat_axis=0, tiled=True)  29 us
    ppermute x6, starting transfers between devices, shifted(): return lax.ppermute(block, axis, route)  25.4 us
    psum x3, blocking collectives, per_device(): squared_entries = lax.psum(jnp.sum(mixed * mixed, axis=1), 'col')  16.4 us
    all_to_all x1, starting transfers between devices, per_device(): lax.all_to_all(pieces, 'dom', split_axis=0, concat_axis=0, tiled=True)  14.6 us
    convert_element_type x5, other arithmetic, per_device(): jnp.where(clamp_mask[:, None] == 1, seed_float, mixed / row_scale[:, None])  12.3 us
  transfers between devices with their start and end apart: 7, of which 7 were waited for; matrix products, arithmetic and copies ran while one was open for 4% of the time, Pallas kernels for 0%

commit v1 on v0

v1 whole, which is shorter than its diff:
```python
import functools

import jax
import jax.numpy as jnp
from jax import lax
from jax.experimental import pallas as pl
from jax.experimental.pallas import tpu as pltpu
from jax.sharding import PartitionSpec as P


ITERS = 3
TILE = 128
TILES = 32
SLOTS = 16
CAP = 4
LATE = 6
EARLY = SLOTS - LATE
ZERO = TILES
COLS = 256

carry_weight = 0.9
norm_eps = 1e-05

VMEM = pl.BlockSpec(memory_space=pltpu.VMEM)
SMEM = pl.BlockSpec(memory_space=pltpu.SMEM)
MIB = 1 << 20


def in_vmem(shape, dtype):
    return pltpu.VMEM(shape, dtype)


def tables_kernel(nt_ref, tile_ref, slot_ref, rest_ref, below_ref, above_ref, place_ref):
    base = nt_ref[0] - TILES

    def clear(j, c):
        place_ref[j] = 0
        return c

    lax.fori_loop(0, 3 * TILES, clear, 0)

    def mark(e, c):
        place_ref[nt_ref[e] - base] = 1
        return c

    lax.fori_loop(0, TILES * SLOTS, mark, 0, unroll=8)
    for q in range(128):
        below_ref[q] = 0
        above_ref[q] = 0

    def name(j, c):
        count_below, count_above = c
        far = j + 2 * TILES
        is_below = place_ref[j]
        is_above = place_ref[far]

        @pl.when(is_below == 1)
        def _():
            below_ref[jnp.minimum(count_below, CAP - 1)] = j

        @pl.when(is_above == 1)
        def _():
            above_ref[jnp.minimum(count_above, CAP - 1)] = j

        place_ref[j] = ZERO + 1 + count_below
        place_ref[far] = ZERO + 1 + CAP + count_above
        place_ref[j + TILES] = j
        return count_below + is_below, count_above + is_above

    lax.fori_loop(0, TILES, name, (0, 0))

    def row(t, total):
        head, tail = t * SLOTS, t * SLOTS + SLOTS - 1
        for k in range(SLOTS):
            off = nt_ref[t * SLOTS + k] - base
            own = ((off >= TILES) & (off < 2 * TILES)).astype(jnp.int32)
            at = jnp.where(own == 1, head, tail)
            tile_ref[at] = place_ref[off]
            slot_ref[at] = t * SLOTS + k
            head = head + own
            tail = tail - (1 - own)
        rest = jnp.maximum(EARLY - (head - t * SLOTS), 0)
        rest_ref[t] = rest
        return total + rest

    rest_ref[TILES] = lax.fori_loop(0, TILES, row, 0)


def tables(nt):
    n = TILES * SLOTS
    i32 = lambda k: jax.ShapeDtypeStruct((k,), jnp.int32)
    return pl.pallas_call(
        tables_kernel,
        out_shape=(i32(n), i32(n), i32(128), i32(128), i32(128)),
        in_specs=[SMEM],
        out_specs=(SMEM,) * 5,
        scratch_shapes=[pltpu.SMEM((3 * TILES,), jnp.int32)],
        compiler_params=pltpu.CompilerParams(vmem_limit_bytes=MIB),
        cost_estimate=pl.CostEstimate(flops=0, bytes_accessed=16 * MIB, transcendentals=0),
        name="tables",
    )(nt)


def stage_kernel(a_ref, clamp_ref, inv_ref, held_ref, v_ref, sem):
    step = 4
    copies = [
        pltpu.make_async_copy(a_ref.at[pl.ds(g * step, step)], v_ref.at[pl.ds(g * step, step)], sem.at[g])
        for g in range(TILES // step)
    ]
    for c in copies:
        c.start()
    lane = lax.broadcasted_iota(jnp.int32, (TILE, TILE), 1)
    inv_ref[...] = jnp.zeros((TILE, TILE), jnp.float32)
    clamp = clamp_ref[...].astype(jnp.float32)
    held_ref[...] = jnp.concatenate([clamp, jnp.zeros((TILE - TILES, TILE), jnp.float32)], axis=0).T
    for g, c in enumerate(copies):
        c.wait()

        def body(u, carry, g=g):
            t = g * step + u
            total = jnp.zeros((TILE, TILE), jnp.float32)
            for k in range(SLOTS):
                total = total + v_ref[t, k].astype(jnp.float32)
            inv = carry_weight / jnp.sum(total, axis=1, keepdims=True)
            inv_ref[...] = jnp.where(lane == t, inv, inv_ref[...])
            return carry

        lax.fori_loop(0, step, body, 0)


def stage(affinity, clamp):
    return pl.pallas_call(
        stage_kernel,
        out_shape=(
            jax.ShapeDtypeStruct((TILE, TILE), jnp.float32),
            jax.ShapeDtypeStruct((TILE, TILE), jnp.float32),
        ),
        in_specs=[pl.BlockSpec(memory_space=pltpu.HBM), VMEM],
        out_specs=(VMEM,) * 2,
        scratch_shapes=[pltpu.VMEM(affinity.shape, jnp.bfloat16), pltpu.SemaphoreType.DMA((TILES // 4,))],
        compiler_params=pltpu.CompilerParams(vmem_limit_bytes=42 * MIB),
        cost_estimate=pl.CostEstimate(flops=TILES * SLOTS * TILE * TILE, bytes_accessed=16 * MIB, transcendentals=0),
        name="stage",
    )(affinity, clamp)


def both_kernel(to_below, to_above, asked):
    for r in range(CAP):
        asked[r] = to_below[r]
        asked[CAP + r] = to_above[r]


def both(to_below, to_above):
    return pl.pallas_call(
        both_kernel,
        out_shape=jax.ShapeDtypeStruct((128,), jnp.int32),
        in_specs=[SMEM] * 2,
        out_specs=SMEM,
        compiler_params=pltpu.CompilerParams(vmem_limit_bytes=MIB),
        name="both",
    )(to_below, to_above)


def pack_sends(send_below_ref, send_above_ref, pool_ref, asked):
    for r in range(CAP):
        send_below_ref[r] = pool_ref[asked[r]]
        send_above_ref[r] = pool_ref[asked[CAP + r]]


def order_kernel(order_ref, asked, own_ref, other_ref, a_ref, pool_ref, send_below_ref, send_above_ref, v_ref, src, dst, sem):
    load = pltpu.make_async_copy(a_ref, v_ref, sem)
    load.start()
    src[:, 0:TILE] = own_ref[...].astype(jnp.float32)
    src[:, TILE:COLS] = other_ref[...].astype(jnp.float32)
    unroll = 32

    def step(i, c):
        base = pl.multiple_of(i * unroll, unroll)
        for u in range(unroll):
            dst[pl.ds(base + u, 1), :] = src[pl.ds(order_ref[base + u], 1), :]
        return c

    lax.fori_loop(0, TILES * TILE // unroll, step, 0)
    pool_ref[0:TILES] = dst[...].astype(jnp.bfloat16).reshape(TILES, TILE, COLS)
    pool_ref[ZERO] = jnp.zeros((TILE, COLS), jnp.bfloat16)
    pack_sends(send_below_ref, send_above_ref, pool_ref, asked)
    load.wait()


POOL = (TILES + 1, TILE, COLS)
SEND = (CAP, TILE, COLS)


def order_rows(order, asked, own, other, affinity):
    return pl.pallas_call(
        order_kernel,
        out_shape=(
            in_vmem(POOL, jnp.bfloat16),
            in_vmem(SEND, jnp.bfloat16),
            in_vmem(SEND, jnp.bfloat16),
            in_vmem(affinity.shape, jnp.bfloat16),
        ),
        in_specs=[SMEM, SMEM, VMEM, VMEM, pl.BlockSpec(memory_space=pltpu.HBM)],
        out_specs=(VMEM,) * 4,
        scratch_shapes=[pltpu.VMEM((TILES * TILE, COLS), jnp.float32)] * 2 + [pltpu.SemaphoreType.DMA],
        compiler_params=pltpu.CompilerParams(vmem_limit_bytes=32 * MIB),
        name="order_rows",
    )(order, asked, own, other, affinity)


def early_kernel(tile_ref, slot_ref, a_ref, pool_ref, acc_ref):
    unroll = 4

    def step(g, c):
        for u in range(unroll):
            t = g * unroll + u
            lhs, rhs = [], []
            for k in range(EARLY):
                tile = tile_ref[t * SLOTS + k]
                lhs.append(a_ref[slot_ref[t * SLOTS + k]])
                rhs.append(pool_ref[jnp.minimum(tile, ZERO)])
            acc_ref[t] = jnp.dot(
                jnp.concatenate(lhs, axis=1), jnp.concatenate(rhs, axis=0), preferred_element_type=jnp.float32
            )
        return c

    lax.fori_loop(0, TILES // unroll, step, 0)


def early(tile, slot, a, pool):
    flops = 2 * TILES * EARLY * TILE * TILE * COLS
    return pl.pallas_call(
        early_kernel,
        out_shape=in_vmem((TILES, TILE, COLS), jnp.float32),
        in_specs=[SMEM, SMEM, VMEM, VMEM],
        out_specs=VMEM,
        compiler_params=pltpu.CompilerParams(vmem_limit_bytes=8 * MIB),
        cost_estimate=pl.CostEstimate(flops=flops, bytes_accessed=16 * MIB, transcendentals=0),
        name="early",
    )(tile, slot, a, pool)


def late_kernel(last, tile_ref, slot_ref, rest_ref, asked, a_ref, acc_in, pool_ref, below_ref, above_ref,
                seed_ref, inv_ref, clamp_ref, acc_ref, *refs):
    if last:
        out_ref, every = refs
    else:
        new_ref, send_below_ref, send_above_ref, every = refs
    every[0 : TILES + 1] = pool_ref[...]
    every[TILES + 1 : TILES + 1 + CAP] = below_ref[...]
    every[TILES + 1 + CAP :] = above_ref[...]

    @pl.when(rest_ref[TILES] > 0)
    def _():
        def row(t, c):
            def one(r, c):
                at = t * SLOTS + EARLY - 1 - r
                acc_ref[t] = acc_ref[t] + jnp.dot(
                    a_ref[slot_ref[at]], every[tile_ref[at]], preferred_element_type=jnp.float32
                )
                return c

            return lax.fori_loop(0, rest_ref[t], one, c)

        lax.fori_loop(0, TILES, row, 0)

    unroll = 4
    lane = lax.broadcasted_iota(jnp.int32, (TILE, TILE), 1)

    def step(g, c):
        for u in range(unroll):
            t = g * unroll + u
            lhs, rhs = [], []
            for k in range(EARLY, SLOTS):
                lhs.append(a_ref[slot_ref[t * SLOTS + k]])
                rhs.append(every[tile_ref[t * SLOTS + k]])
            spread = acc_ref[t] + jnp.dot(
                jnp.concatenate(lhs, axis=1), jnp.concatenate(rhs, axis=0), preferred_element_type=jnp.float32
            )
            mine = lane == t
            inv = jnp.sum(jnp.where(mine, inv_ref[...], 0.0), axis=1, keepdims=True)
            held = jnp.sum(jnp.where(mine, clamp_ref[...], 0.0), axis=1, keepdims=True)
            seed = seed_ref[t].astype(jnp.float32)
            mixed = spread * inv + (1.0 - carry_weight) * seed
            mean = jnp.sum(mixed * mixed, axis=1, keepdims=True) * (1.0 / COLS)
            scaled = mixed * lax.rsqrt(mean + norm_eps)
            new = jnp.where(held > 0.5, seed, scaled).astype(jnp.bfloat16)
            if last:
                out_ref[t] = new[:, 0:TILE]
            else:
                new_ref[t] = new
        return c

    lax.fori_loop(0, TILES // unroll, step, 0)
    if not last:
        new_ref[ZERO] = jnp.zeros((TILE, COLS), jnp.bfloat16)
        pack_sends(send_below_ref, send_above_ref, new_ref, asked)


def late(last, tile, slot, rest, asked, a, acc, pool, below, above, seed, inv, clamp):
    acc_out = in_vmem((TILES, TILE, COLS), jnp.float32)
    if last:
        outs = (acc_out, jax.ShapeDtypeStruct((TILES, TILE, TILE), jnp.bfloat16))
    else:
        outs = (acc_out, in_vmem(POOL, jnp.bfloat16), in_vmem(SEND, jnp.bfloat16), in_vmem(SEND, jnp.bfloat16))
    return pl.pallas_call(
        functools.partial(late_kernel, last),
        out_shape=outs,
        in_specs=[SMEM] * 4 + [VMEM] * 8,
        out_specs=(VMEM,) * len(outs),
        input_output_aliases={5: 0},
        scratch_shapes=[pltpu.VMEM((TILES + 1 + 2 * CAP, TILE, COLS), jnp.bfloat16)],
        compiler_params=pltpu.CompilerParams(vmem_limit_bytes=8 * MIB),
        name="late_last" if last else "late",
    )(tile, slot, rest, asked, a, acc, pool, below, above, seed, inv, clamp)[1:]


def shifted(block, distance):
    devices = range(lax.axis_size("dom"))
    route = [(i - distance, i) for i in devices if i - distance in devices]
    return lax.ppermute(block, "dom", route)


def per_device(seed_data, dataset_order, affinity, neighbour_tiles, clamp_mask):
    part_count = lax.axis_size("dom")
    cell_count, slab = seed_data.shape
    pieces = seed_data.reshape(part_count, cell_count // part_count, slab)
    own = lax.all_to_all(pieces, "dom", split_axis=0, concat_axis=0, tiled=True).reshape(cell_count, slab)
    tile, slot, rest, need_below, need_above = tables(neighbour_tiles.reshape(-1))
    to_above = shifted(need_below, -1)
    to_below = shifted(need_above, 1)
    asked = both(to_below, to_above)
    inv, clamp = stage(affinity, clamp_mask.reshape(TILES, TILE))
    other = lax.ppermute(own, "col", [(0, 1), (1, 0)])
    affinity = affinity.reshape(TILES * SLOTS, TILE, TILE)
    pool, send_below, send_above, a = order_rows(dataset_order.reshape(-1), asked, own, other, affinity)
    seed = pool
    for iteration in range(ITERS):
        above = shifted(send_below, -1)
        below = shifted(send_above, 1)
        acc = early(tile, slot, a, pool)
        last = iteration == ITERS - 1
        result = late(last, tile, slot, rest, asked, a, acc, pool, below, above, seed, inv, clamp)
        if last:
            return result[0].reshape(cell_count, slab)
        pool, send_below, send_above = result


def solution(mesh):
    return jax.shard_map(
        per_device,
        mesh=mesh,
        in_specs=(
            P("dom", "col"),
            P("dom", None),
            P("dom", None, None, None),
            P("dom", None),
            P("dom"),
        ),
        out_specs=P("dom", "col"),
        check_vma=False,
    )
```

time: 271 us -> 152 us (0.56)
  the two profiles are of different devices: /device:TPU:33 before, /device:TPU:30 now
where the time goes in v1:
time: 152 us; the launch traced here: 151 us
  Pallas kernels  58.8 us (39%)
  blocking collectives  42.6 us (28%)
  starting transfers between devices  29.4 us (19%)
  waiting for transfers between devices  18.4 us (12%)
  local copies, waits for them, and re-layouts  1.57 us (1%)
    all_to_all x1, blocking collectives, per_device(): lax.all_to_all(pieces, 'dom', split_axis=0, concat_axis=0, tiled=True)  42.6 us
    ppermute x8, starting transfers between devices, shifted(): return lax.ppermute(block, 'dom', route)  29.4 us
    ppermute x8, waiting for transfers between devices, shifted(): return lax.ppermute(block, 'dom', route)  18.4 us
    pallas_call x3, Pallas kernels, late(): pl.pallas_call(functools.partial(late_kernel, last), out_shape=outs, in_s...  16.2 us
    pallas_call x1, Pallas kernels, order_rows(): pl.pallas_call(order_kernel, out_shape=(in_vmem(POOL, jnp.bfloat16), in_v...  14.6 us
    pallas_call x3, Pallas kernels, early(): pl.pallas_call(early_kernel, out_shape=in_vmem((TILES, TILE, COLS), jnp.f...  14.2 us
    pallas_call x1, Pallas kernels, stage(): pl.pallas_call(stage_kernel, out_shape=(jax.ShapeDtypeStruct((TILE, TILE)...  6.69 us
    pallas_call x1, Pallas kernels, tables(): pl.pallas_call(tables_kernel, out_shape=(i32(n), i32(n), i32(128), i32(12...  5.99 us
  transfers between devices with their start and end apart: 9, of which 3 were waited for; matrix products, arithmetic and copies ran while one was open for 1% of the time, Pallas kernels for 19%

profile of v1, /device:TPU:30, one launch (start us, length us, event | category | flops | bytes accessed | tf_op | source)
XLA Modules:
  0.0 151.0 jit_solution(5559977487875790515)
XLA Ops:
  0.0 42.6 %all_to_all.5 = bf16[128,32,128]{2,1,0:T(8,128)(2,1)S(1)} all-to-all(bf16[128,32,128]{2,1,0:T(8,128)(2,1)} %bitcast.11), channel_id=1, replica_groups=mesh['dom'=128,'col'=2] {'dom'}, dimensions={0} | all-to-all | bytes 2097152 | tf_op jit(solution)/shard_map/all_to_all | solution.py:328
  42.6 0.8 copy.9
  43.5 6.0 %tables.1 = (s32[512]{0:T(512)S(1)}, s32[512]{0:T(512)S(1)}, s32[128]{0:T(128)S(1)}, s32[128]{0:T(128)S(1)}, s32[128]{0:T(128)S(1)}) custom-call(s32[512]{0:T(512)S(1)} %reshape.21.nt_ref), custom_call_target="tpu_custom_call" | custom-call | bytes 16777216 | tf_op jit(solution)/shard_map/tables/pallas_call | solution.py:92
  49.5 7.2 %collective-permute-start = (s32[128]{0:T(128)S(1)}, s32[128]{0:T(128)S(1)}, u32[]{:S(2)}, u32[]{:S(2)}) collective-permute-start(s32[128]{0:T(128)S(1)} %get-tuple-element.26), channel_id=1, source_target_pairs={{0,2},{2,4},{4,6},{6,8},{8,10},{10,12},{12,14},{14,16},{16,18},{18... | collective-permute-start | bytes 1544 | tf_op jit(solution)/shard_map/ppermute | solution.py:321
  56.6 1.9 %collective-permute-start.1 = (s32[128]{0:T(128)S(1)}, s32[128]{0:T(128)S(1)}, u32[]{:S(2)}, u32[]{:S(2)}) collective-permute-start(s32[128]{0:T(128)S(1)} %get-tuple-element.27), channel_id=1, source_target_pairs={{2,0},{4,2},{6,4},{8,6},{10,8},{12,10},{14,12},{16,14},{18,16},{20... | collective-permute-start | bytes 1544 | tf_op jit(solution)/shard_map/ppermute | solution.py:321
  58.6 7.7 %collective-permute-done.1.to_above = s32[128]{0:T(128)S(1)} collective-permute-done((s32[128]{0:T(128)S(1)}, s32[128]{0:T(128)S(1)}, u32[]{:S(2)}, u32[]{:S(2)}) %collective-permute-start.1) | collective-permute-done | bytes 544 | tf_op jit(solution)/shard_map/ppermute | solution.py:321
  66.3 1.1 both.1.asked
  67.5 0.7 copy-done
  68.2 14.6 %order_rows.1 = (bf16[33,128,256]{2,1,0:T(8,128)(2,1)S(1)}, bf16[4,128,256]{2,1,0:T(8,128)(2,1)S(1)}, bf16[4,128,256]{2,1,0:T(8,128)(2,1)S(1)}, bf16[512,128,128]{2,1,0:T(8,128)(2,1)S(1)}) custom-call(s32[4096]{0:T(1024)S(1)} %bitcast.8, s32[128]{0:T(128)S(1)} %both.1.asked, bf16[4096,128]{1,0:T(8,128)(2,1)S(1)} %bitcast.7, ...), custom_call_target="tpu_custom_call" | custom-call | tf_op jit(solution)/shard_map/order_rows/pallas_call | solution.py:195
  82.8 1.9 %collective-permute-start.3 = (bf16[4,128,256]{2,1,0:T(8,128)(2,1)S(1)}, bf16[4,128,256]{2,1,0:T(8,128)(2,1)S(1)}, u32[]{:S(2)}, u32[]{:S(2)}) collective-permute-start(bf16[4,128,256]{2,1,0:T(8,128)(2,1)S(1)} %get-tuple-element.30), channel_id=1, source_target_pairs={{0,2},{2,4},{4,6},{6,8},{8,10},{10,12},{12,14},{14,16},{16,18},{18... | collective-permute-start | bytes 786440 | tf_op jit(solution)/shard_map/ppermute | solution.py:321
  84.7 3.9 %collective-permute-start.4 = (bf16[4,128,256]{2,1,0:T(8,128)(2,1)S(1)}, bf16[4,128,256]{2,1,0:T(8,128)(2,1)S(1)}, u32[]{:S(2)}, u32[]{:S(2)}) collective-permute-start(bf16[4,128,256]{2,1,0:T(8,128)(2,1)S(1)} %get-tuple-element.31), channel_id=1, source_target_pairs={{2,0},{4,2},{6,4},{8,6},{10,8},{12,10},{14,12},{16,14},{18,16},{20... | collective-permute-start | bytes 786440 | tf_op jit(solution)/shard_map/ppermute | solution.py:321
  88.7 6.7 %stage.1 = (f32[128,128]{1,0:T(8,128)S(1)}, f32[128,128]{1,0:T(8,128)S(1)}) custom-call(bf16[32,16,128,128]{3,2,1,0:T(8,128)(2,1)} %a_ref.1, s32[32,128]{1,0:T(8,128)S(1)} %bitcast.9), custom_call_target="tpu_custom_call" | custom-call | flops 8388608 | bytes 16777216 | tf_op jit(solution)/shard_map/stage/pallas_call | solution.py:132
  95.4 4.8 %early.3.acc_in = f32[32,128,256]{2,1,0:T(8,128)S(1)} custom-call(s32[512]{0:T(512)S(1)} %get-tuple-element.23.tile_ref, s32[512]{0:T(512)S(1)} %get-tuple-element.24.slot_ref, bf16[512,128,128]{2,1,0:T(8,128)(2,1)S(1)} %get-tuple-element.28.a_ref, bf16[33,128,256]{2,1,0:T(8,128)(2,1)S(1)} %get-tuple-element.29.pool_ref.seed_ref), custom_call_target="tpu_custom_call" | custom-call | flops 2684354560 | bytes 16777216 | tf_op jit(solution)/shard_map/early/pallas_call | solution.py:232
  100.2 5.1 %late.2 = (f32[32,128,256]{2,1,0:T(8,128)S(1)}, bf16[33,128,256]{2,1,0:T(8,128)(2,1)S(1)}, bf16[4,128,256]{2,1,0:T(8,128)(2,1)S(1)}, bf16[4,128,256]{2,1,0:T(8,128)(2,1)S(1)}) custom-call(s32[512]{0:T(512)S(1)} %get-tuple-element.23.tile_ref, s32[512]{0:T(512)S(1)} %get-tuple-element.24.slot_ref, ...), custom_call_target="tpu_custom_call", output_to_operand_aliasing={{0}: (5, {})} | custom-call | tf_op jit(solution)/shard_map/late/pallas_call | solution.py:306
  105.3 6.7 %collective-permute-start.5 = (bf16[4,128,256]{2,1,0:T(8,128)(2,1)S(1)}, bf16[4,128,256]{2,1,0:T(8,128)(2,1)S(1)}, u32[]{:S(2)}, u32[]{:S(2)}) collective-permute-start(bf16[4,128,256]{2,1,0:T(8,128)(2,1)S(1)} %get-tuple-element.35), channel_id=1, source_target_pairs={{0,2},{2,4},{4,6},{6,8},{8,10},{10,12},{12,14},{14,16},{16,18},{18... | collective-permute-start | bytes 786440 | tf_op jit(solution)/shard_map/ppermute | solution.py:321
  112.0 1.9 %collective-permute-start.6 = (bf16[4,128,256]{2,1,0:T(8,128)(2,1)S(1)}, bf16[4,128,256]{2,1,0:T(8,128)(2,1)S(1)}, u32[]{:S(2)}, u32[]{:S(2)}) collective-permute-start(bf16[4,128,256]{2,1,0:T(8,128)(2,1)S(1)} %get-tuple-element.36), channel_id=1, source_target_pairs={{2,0},{4,2},{6,4},{8,6},{10,8},{12,10},{14,12},{16,14},{18,16},{20... | collective-permute-start | bytes 786440 | tf_op jit(solution)/shard_map/ppermute | solution.py:321
  114.0 4.8 %early.4.acc_in = f32[32,128,256]{2,1,0:T(8,128)S(1)} custom-call(s32[512]{0:T(512)S(1)} %get-tuple-element.23.tile_ref, s32[512]{0:T(512)S(1)} %get-tuple-element.24.slot_ref, bf16[512,128,128]{2,1,0:T(8,128)(2,1)S(1)} %get-tuple-element.28.a_ref, bf16[33,128,256]{2,1,0:T(8,128)(2,1)S(1)} %get-tuple-element.34.pool_ref), custom_call_target="tpu_custom_call" | custom-call | flops 2684354560 | bytes 16777216 | tf_op jit(solution)/shard_map/early/pallas_call | solution.py:232
  118.7 6.1 %collective-permute-done.6.above_ref = bf16[4,128,256]{2,1,0:T(8,128)(2,1)S(1)} collective-permute-done((bf16[4,128,256]{2,1,0:T(8,128)(2,1)S(1)}, bf16[4,128,256]{2,1,0:T(8,128)(2,1)S(1)}, u32[]{:S(2)}, u32[]{:S(2)}) %collective-permute-start.6) | collective-permute-done | bytes 262176 | tf_op jit(solution)/shard_map/ppermute | solution.py:321
  124.8 5.1 %late.3 = (f32[32,128,256]{2,1,0:T(8,128)S(1)}, bf16[33,128,256]{2,1,0:T(8,128)(2,1)S(1)}, bf16[4,128,256]{2,1,0:T(8,128)(2,1)S(1)}, bf16[4,128,256]{2,1,0:T(8,128)(2,1)S(1)}) custom-call(s32[512]{0:T(512)S(1)} %get-tuple-element.23.tile_ref, s32[512]{0:T(512)S(1)} %get-tuple-element.24.slot_ref, ...), custom_call_target="tpu_custom_call", output_to_operand_aliasing={{0}: (5, {})} | custom-call | tf_op jit(solution)/shard_map/late/pallas_call | solution.py:306
  130.0 2.6 %collective-permute-start.7 = (bf16[4,128,256]{2,1,0:T(8,128)(2,1)S(1)}, bf16[4,128,256]{2,1,0:T(8,128)(2,1)S(1)}, u32[]{:S(2)}, u32[]{:S(2)}) collective-permute-start(bf16[4,128,256]{2,1,0:T(8,128)(2,1)S(1)} %get-tuple-element.38), channel_id=1, source_target_pairs={{0,2},{2,4},{4,6},{6,8},{8,10},{10,12},{12,14},{14,16},{16,18},{18... | collective-permute-start | bytes 786440 | tf_op jit(solution)/shard_map/ppermute | solution.py:321
  132.6 3.2 %collective-permute-start.8 = (bf16[4,128,256]{2,1,0:T(8,128)(2,1)S(1)}, bf16[4,128,256]{2,1,0:T(8,128)(2,1)S(1)}, u32[]{:S(2)}, u32[]{:S(2)}) collective-permute-start(bf16[4,128,256]{2,1,0:T(8,128)(2,1)S(1)} %get-tuple-element.39), channel_id=1, source_target_pairs={{2,0},{4,2},{6,4},{8,6},{10,8},{12,10},{14,12},{16,14},{18,16},{20... | collective-permute-start | bytes 786440 | tf_op jit(solution)/shard_map/ppermute | solution.py:321
  135.8 4.7 %early.5.acc_in = f32[32,128,256]{2,1,0:T(8,128)S(1)} custom-call(s32[512]{0:T(512)S(1)} %get-tuple-element.23.tile_ref, s32[512]{0:T(512)S(1)} %get-tuple-element.24.slot_ref, bf16[512,128,128]{2,1,0:T(8,128)(2,1)S(1)} %get-tuple-element.28.a_ref, bf16[33,128,256]{2,1,0:T(8,128)(2,1)S(1)} %get-tuple-element.37.pool_ref), custom_call_target="tpu_custom_call" | custom-call | flops 2684354560 | bytes 16777216 | tf_op jit(solution)/shard_map/early/pallas_call | solution.py:232
  140.6 4.5 %collective-permute-done.8.above_ref = bf16[4,128,256]{2,1,0:T(8,128)(2,1)S(1)} collective-permute-done((bf16[4,128,256]{2,1,0:T(8,128)(2,1)S(1)}, bf16[4,128,256]{2,1,0:T(8,128)(2,1)S(1)}, u32[]{:S(2)}, u32[]{:S(2)}) %collective-permute-start.8) | collective-permute-done | bytes 262176 | tf_op jit(solution)/shard_map/ppermute | solution.py:321
  145.1 5.9 %late_last.1 = (f32[32,128,256]{2,1,0:T(8,128)S(1)}, bf16[32,128,128]{2,1,0:T(8,128)(2,1)}) custom-call(s32[512]{0:T(512)S(1)} %get-tuple-element.23.tile_ref, s32[512]{0:T(512)S(1)} %get-tuple-element.24.slot_ref, s32[128]{0:T(128)S(1)} %get-tuple-element.25.rest_ref, s32[128]{0:T(128)S(1)} %both.1.asked, ...), custom_call_target="tpu_custom_call", output_to_operand_aliasing={{0}: (5, {})} | custom-call | tf_op jit(solution)/shard_map/late_last/pallas_call | solution.py:306
  (11 shorter events, 0.1 us)
Async XLA Ops:
  42.6 24.9 %collective-permute-start.2 = (bf16[4096,128]{1,0:T(8,128)(2,1)S(1)}, bf16[4096,128]{1,0:T(8,128)(2,1)S(1)}, u32[]{:S(2)}, u32[]{:S(2)}) collective-permute-start(bf16[4096,128]{1,0:T(8,128)(2,1)S(1)} %bitcast.6), channel_id=1, source_target_pairs={{0,1},{1,0},{2,3},{3,2},{4,5},{5,4},{6,7},{7,6},{8,9},{9,8},{10,11... | collective-permute-start | bytes 3145736 | tf_op jit(solution)/shard_map/ppermute | solution.py:334
  49.5 9.1 %collective-permute-start = (s32[128]{0:T(128)S(1)}, s32[128]{0:T(128)S(1)}, u32[]{:S(2)}, u32[]{:S(2)}) collective-permute-start(s32[128]{0:T(128)S(1)} %get-tuple-element.26), channel_id=1, source_target_pairs={{0,2},{2,4},{4,6},{6,8},{8,10},{10,12},{12,14},{14,16},{16,18},{18... | collective-permute-start | bytes 1544 | tf_op jit(solution)/shard_map/ppermute | solution.py:321
  56.6 9.7 %collective-permute-start.1 = (s32[128]{0:T(128)S(1)}, s32[128]{0:T(128)S(1)}, u32[]{:S(2)}, u32[]{:S(2)}) collective-permute-start(s32[128]{0:T(128)S(1)} %get-tuple-element.27), channel_id=1, source_target_pairs={{2,0},{4,2},{6,4},{8,6},{10,8},{12,10},{14,12},{16,14},{18,16},{20... | collective-permute-start | bytes 1544 | tf_op jit(solution)/shard_map/ppermute | solution.py:321
  67.5 0.7 copy-start
  68.2 20.5 %copy-start.1 = (s32[4096]{0:T(1024)S(1)}, s32[4096]{0:T(1024)}, u32[]{:S(2)}) copy-start(s32[4096]{0:T(1024)} %param.9) | copy-start | bytes 49156
  82.8 17.3 %collective-permute-start.3 = (bf16[4,128,256]{2,1,0:T(8,128)(2,1)S(1)}, bf16[4,128,256]{2,1,0:T(8,128)(2,1)S(1)}, u32[]{:S(2)}, u32[]{:S(2)}) collective-permute-start(bf16[4,128,256]{2,1,0:T(8,128)(2,1)S(1)} %get-tuple-element.30), channel_id=1, source_target_pairs={{0,2},{2,4},{4,6},{6,8},{8,10},{10,12},{12,14},{14,16},{16,18},{18... | collective-permute-start | bytes 786440 | tf_op jit(solution)/shard_map/ppermute | solution.py:321
  84.7 15.4 %collective-permute-start.4 = (bf16[4,128,256]{2,1,0:T(8,128)(2,1)S(1)}, bf16[4,128,256]{2,1,0:T(8,128)(2,1)S(1)}, u32[]{:S(2)}, u32[]{:S(2)}) collective-permute-start(bf16[4,128,256]{2,1,0:T(8,128)(2,1)S(1)} %get-tuple-element.31), channel_id=1, source_target_pairs={{2,0},{4,2},{6,4},{8,6},{10,8},{12,10},{14,12},{16,14},{18,16},{20... | collective-permute-start | bytes 786440 | tf_op jit(solution)/shard_map/ppermute | solution.py:321
  105.3 13.4 %collective-permute-start.5 = (bf16[4,128,256]{2,1,0:T(8,128)(2,1)S(1)}, bf16[4,128,256]{2,1,0:T(8,128)(2,1)S(1)}, u32[]{:S(2)}, u32[]{:S(2)}) collective-permute-start(bf16[4,128,256]{2,1,0:T(8,128)(2,1)S(1)} %get-tuple-element.35), channel_id=1, source_target_pairs={{0,2},{2,4},{4,6},{6,8},{8,10},{10,12},{12,14},{14,16},{16,18},{18... | collective-permute-start | bytes 786440 | tf_op jit(solution)/shard_map/ppermute | solution.py:321
  112.0 12.8 %collective-permute-start.6 = (bf16[4,128,256]{2,1,0:T(8,128)(2,1)S(1)}, bf16[4,128,256]{2,1,0:T(8,128)(2,1)S(1)}, u32[]{:S(2)}, u32[]{:S(2)}) collective-permute-start(bf16[4,128,256]{2,1,0:T(8,128)(2,1)S(1)} %get-tuple-element.36), channel_id=1, source_target_pairs={{2,0},{4,2},{6,4},{8,6},{10,8},{12,10},{14,12},{16,14},{18,16},{20... | collective-permute-start | bytes 786440 | tf_op jit(solution)/shard_map/ppermute | solution.py:321
  130.0 10.6 %collective-permute-start.7 = (bf16[4,128,256]{2,1,0:T(8,128)(2,1)S(1)}, bf16[4,128,256]{2,1,0:T(8,128)(2,1)S(1)}, u32[]{:S(2)}, u32[]{:S(2)}) collective-permute-start(bf16[4,128,256]{2,1,0:T(8,128)(2,1)S(1)} %get-tuple-element.38), channel_id=1, source_target_pairs={{0,2},{2,4},{4,6},{6,8},{8,10},{10,12},{12,14},{14,16},{16,18},{18... | collective-permute-start | bytes 786440 | tf_op jit(solution)/shard_map/ppermute | solution.py:321
  132.6 12.5 %collective-permute-start.8 = (bf16[4,128,256]{2,1,0:T(8,128)(2,1)S(1)}, bf16[4,128,256]{2,1,0:T(8,128)(2,1)S(1)}, u32[]{:S(2)}, u32[]{:S(2)}) collective-permute-start(bf16[4,128,256]{2,1,0:T(8,128)(2,1)S(1)} %get-tuple-element.39), channel_id=1, source_target_pairs={{2,0},{4,2},{6,4},{8,6},{10,8},{12,10},{14,12},{16,14},{18,16},{20... | collective-permute-start | bytes 786440 | tf_op jit(solution)/shard_map/ppermute | solution.py:321

commit v2 on v1

v2 whole, which is shorter than its diff:
```python
import jax
import jax.numpy as jnp
from jax import lax
from jax.experimental import pallas as pl
from jax.experimental.pallas import tpu as pltpu
from jax.sharding import PartitionSpec as P


ITERS = 3
TILE = 128
TILES = 32
SLOTS = 16
SLOT_AT = TILES * SLOTS
CAP = 4
EARLY = 10
REST_AT = 2 * TILES * SLOTS
ZERO = TILES
COLS = 256

carry_weight = 0.9
norm_eps = 1e-05

VMEM = pl.BlockSpec(memory_space=pltpu.VMEM)
SMEM = pl.BlockSpec(memory_space=pltpu.SMEM)
MIB = 1 << 20


def in_vmem(shape, dtype):
    return pltpu.VMEM(shape, dtype)


def tables_kernel(nt_ref, core_ref, table_ref, need_ref, place_ref):
    base = nt_ref[0] - TILES
    direct = jnp.where(core_ref[0] == 0, 2 * TILES, 0)
    swapped = 2 * TILES - direct

    def clear(j, c):
        place_ref[j] = 0
        return c

    lax.fori_loop(0, 3 * TILES, clear, 0)

    def mark(e, c):
        place_ref[nt_ref[e] - base] = 1
        return c

    lax.fori_loop(0, TILES * SLOTS, mark, 0, unroll=8)
    for q in range(128):
        need_ref[q] = 0

    def name(j, c):
        count_direct, count_swapped = c
        is_direct = place_ref[direct + j]
        is_swapped = place_ref[swapped + j]

        @pl.when(is_direct == 1)
        def _():
            need_ref[jnp.minimum(count_direct, CAP - 1)] = j

        place_ref[direct + j] = ZERO + 1 + count_direct
        place_ref[swapped + j] = ZERO + 1 + CAP + count_swapped
        place_ref[j + TILES] = j
        return count_direct + is_direct, count_swapped + is_swapped

    lax.fori_loop(0, TILES, name, (0, 0))

    def row(t, total):
        head, tail = t * SLOTS, t * SLOTS + SLOTS - 1
        for k in range(SLOTS):
            off = nt_ref[t * SLOTS + k] - base
            own = ((off >= TILES) & (off < 2 * TILES)).astype(jnp.int32)
            at = jnp.where(own == 1, head, tail)
            table_ref[at] = place_ref[off]
            table_ref[SLOT_AT + at] = t * SLOTS + k
            head = head + own
            tail = tail - (1 - own)
        rest = jnp.maximum(EARLY - (head - t * SLOTS), 0)
        table_ref[REST_AT + t] = rest
        return total + rest

    table_ref[REST_AT + TILES] = lax.fori_loop(0, TILES, row, 0)


def tables(nt, core):
    i32 = lambda k: jax.ShapeDtypeStruct((k,), jnp.int32)
    return pl.pallas_call(
        tables_kernel,
        out_shape=(i32(REST_AT + 128), i32(128)),
        in_specs=[SMEM] * 2,
        out_specs=(SMEM,) * 2,
        scratch_shapes=[pltpu.SMEM((3 * TILES,), jnp.int32)],
        compiler_params=pltpu.CompilerParams(vmem_limit_bytes=MIB),
        cost_estimate=pl.CostEstimate(flops=0, bytes_accessed=16 * MIB, transcendentals=0),
        name="tables",
    )(nt, core)


def stage_kernel(a_ref, clamp_ref, inv_ref, held_ref, v_ref, sem):
    step = 4
    copies = [
        pltpu.make_async_copy(a_ref.at[pl.ds(g * step, step)], v_ref.at[pl.ds(g * step, step)], sem.at[g])
        for g in range(TILES // step)
    ]
    for c in copies:
        c.start()
    lane = lax.broadcasted_iota(jnp.int32, (TILE, TILE), 1)
    inv_ref[...] = jnp.zeros((TILE, TILE), jnp.float32)
    clamp = clamp_ref[...].astype(jnp.float32)
    held_ref[...] = jnp.concatenate([clamp, jnp.zeros((TILE - TILES, TILE), jnp.float32)], axis=0).T
    for g, c in enumerate(copies):
        c.wait()

        def body(u, carry, g=g):
            t = g * step + u
            total = jnp.zeros((TILE, TILE), jnp.float32)
            for k in range(SLOTS):
                total = total + v_ref[t, k].astype(jnp.float32)
            inv = carry_weight / jnp.sum(total, axis=1, keepdims=True)
            inv_ref[...] = jnp.where(lane == t, inv, inv_ref[...])
            return carry

        lax.fori_loop(0, step, body, 0)


def stage(affinity, clamp):
    return pl.pallas_call(
        stage_kernel,
        out_shape=(
            jax.ShapeDtypeStruct((TILE, TILE), jnp.float32),
            jax.ShapeDtypeStruct((TILE, TILE), jnp.float32),
        ),
        in_specs=[pl.BlockSpec(memory_space=pltpu.HBM), VMEM],
        out_specs=(VMEM,) * 2,
        scratch_shapes=[pltpu.VMEM(affinity.shape, jnp.bfloat16), pltpu.SemaphoreType.DMA((TILES // 4,))],
        compiler_params=pltpu.CompilerParams(vmem_limit_bytes=42 * MIB),
        cost_estimate=pl.CostEstimate(flops=TILES * SLOTS * TILE * TILE, bytes_accessed=16 * MIB, transcendentals=0),
        name="stage",
    )(affinity, clamp)


POOL = (TILES + 1, TILE, COLS)
HALF = (TILES + 1, TILE, TILE)
SEND = (CAP, TILE, COLS)


def order_kernel(order_ref, own_ref, a_ref, half_ref, v_ref, src, dst, sem):
    load = pltpu.make_async_copy(a_ref, v_ref, sem)
    load.start()
    src[...] = own_ref[...].astype(jnp.float32)
    unroll = 64

    def step(i, c):
        base = pl.multiple_of(i * unroll, unroll)
        for u in range(unroll):
            dst[pl.ds(base + u, 1), :] = src[pl.ds(order_ref[base + u], 1), :]
        return c

    lax.fori_loop(0, TILES * TILE // unroll, step, 0)
    half_ref[0:TILES] = dst[...].astype(jnp.bfloat16).reshape(TILES, TILE, TILE)
    half_ref[ZERO] = jnp.zeros((TILE, TILE), jnp.bfloat16)
    load.wait()


def order_rows(order, own, affinity):
    return pl.pallas_call(
        order_kernel,
        out_shape=(in_vmem(HALF, jnp.bfloat16), in_vmem(affinity.shape, jnp.bfloat16)),
        in_specs=[SMEM, VMEM, pl.BlockSpec(memory_space=pltpu.HBM)],
        out_specs=(VMEM,) * 2,
        scratch_shapes=[pltpu.VMEM((TILES * TILE, TILE), jnp.float32)] * 2 + [pltpu.SemaphoreType.DMA],
        compiler_params=pltpu.CompilerParams(vmem_limit_bytes=32 * MIB),
        name="order_rows",
    )(order, own, affinity)


def labels_of(refs, tile):
    parts = [ref[tile] for ref in refs]
    return parts[0] if len(parts) == 1 else jnp.concatenate(parts, axis=1)


def pack_kernel(asked, *refs):
    for r in range(CAP):
        refs[-1][r] = labels_of(refs[:-1], asked[r])


def pack(asked, labels):
    return pl.pallas_call(
        pack_kernel,
        out_shape=in_vmem(SEND, jnp.bfloat16),
        in_specs=[SMEM] + [VMEM] * len(labels),
        out_specs=VMEM,
        compiler_params=pltpu.CompilerParams(vmem_limit_bytes=MIB),
        name="pack",
    )(asked, *labels)


def early_kernel(table, a_ref, *refs):
    acc_ref, labels = refs[-1], refs[:-1]
    unroll = 4

    def step(g, c):
        for u in range(unroll):
            t = g * unroll + u
            lhs, rhs = [], []
            for k in range(EARLY):
                lhs.append(a_ref[table[SLOT_AT + t * SLOTS + k]])
                rhs.append(labels_of(labels, jnp.minimum(table[t * SLOTS + k], ZERO)))
            acc_ref[t] = jnp.dot(
                jnp.concatenate(lhs, axis=1), jnp.concatenate(rhs, axis=0), preferred_element_type=jnp.float32
            )
        return c

    lax.fori_loop(0, TILES // unroll, step, 0)


def early(table, a, labels):
    flops = 2 * TILES * EARLY * TILE * TILE * COLS
    return pl.pallas_call(
        early_kernel,
        out_shape=in_vmem((TILES, TILE, COLS), jnp.float32),
        in_specs=[SMEM] + [VMEM] * (1 + len(labels)),
        out_specs=VMEM,
        compiler_params=pltpu.CompilerParams(vmem_limit_bytes=8 * MIB),
        cost_estimate=pl.CostEstimate(flops=flops, bytes_accessed=16 * MIB, transcendentals=0),
        name="early",
    )(table, a, *labels)


def gather_pool(every, labels, direct_ref, swapped_ref):
    width = COLS // len(labels)
    for p, ref in enumerate(labels):
        every[0 : TILES + 1, :, p * width : (p + 1) * width] = ref[...]
    every[TILES + 1 : TILES + 1 + CAP] = direct_ref[...]
    every[TILES + 1 + CAP :, :, :TILE] = swapped_ref[:, :, TILE:]
    every[TILES + 1 + CAP :, :, TILE:] = swapped_ref[:, :, :TILE]


def add_rest(table, a_ref, every, acc_ref):
    @pl.when(table[REST_AT + TILES] > 0)
    def _():
        def row(t, c):
            def one(r, c):
                at = t * SLOTS + EARLY - 1 - r
                acc_ref[t] = acc_ref[t] + jnp.dot(
                    a_ref[table[SLOT_AT + at]], every[table[at]], preferred_element_type=jnp.float32
                )
                return c

            return lax.fori_loop(0, table[REST_AT + t], one, c)

        lax.fori_loop(0, TILES, row, 0)


def new_labels(table, a_ref, every, acc_ref, inv_ref, held_ref, seeds, t, width):
    lhs, rhs = [], []
    for k in range(EARLY, SLOTS):
        lhs.append(a_ref[table[SLOT_AT + t * SLOTS + k]])
        rhs.append(every[table[t * SLOTS + k]])
    spread = acc_ref[t] + jnp.dot(
        jnp.concatenate(lhs, axis=1), jnp.concatenate(rhs, axis=0), preferred_element_type=jnp.float32
    )
    mine = lax.broadcasted_iota(jnp.int32, (TILE, TILE), 1) == t
    inv = jnp.sum(jnp.where(mine, inv_ref[...], 0.0), axis=1, keepdims=True)
    held = jnp.sum(jnp.where(mine, held_ref[...], 0.0), axis=1, keepdims=True)
    seed = jnp.concatenate([ref[t] for ref in seeds], axis=1).astype(jnp.float32)
    mixed = spread * inv + (1.0 - carry_weight) * seed
    square = mixed * mixed
    mean = jnp.sum(square[:, :TILE] + square[:, TILE:], axis=1, keepdims=True) * (1.0 / COLS)
    scaled = mixed[:, :width] * lax.rsqrt(mean + norm_eps)
    return jnp.where(held > 0.5, seed[:, :width], scaled).astype(jnp.bfloat16)


def asked_kernel(table, asked, a_ref, acc_in, direct_ref, swapped_ref, inv_ref, held_ref, *refs):
    labels, seeds, (acc_ref, every, send_ref) = refs[:-5], refs[-5:-3], refs[-3:]
    gather_pool(every, labels, direct_ref, swapped_ref)
    add_rest(table, a_ref, every, acc_ref)
    for r in range(CAP):
        send_ref[r] = new_labels(table, a_ref, every, acc_ref, inv_ref, held_ref, seeds, asked[r], COLS)


def asked_tiles(table, asked, a, acc, direct, swapped, inv, held, labels, seeds):
    return pl.pallas_call(
        asked_kernel,
        out_shape=(
            in_vmem((TILES, TILE, COLS), jnp.float32),
            in_vmem(EVERY, jnp.bfloat16),
            in_vmem(SEND, jnp.bfloat16),
        ),
        in_specs=[SMEM] * 2 + [VMEM] * (6 + len(labels) + len(seeds)),
        out_specs=(VMEM,) * 3,
        input_output_aliases={3: 0},
        compiler_params=pltpu.CompilerParams(vmem_limit_bytes=4 * MIB),
        name="asked_tiles",
    )(table, asked, a, acc, direct, swapped, inv, held, *labels, *seeds)


EVERY = (TILES + 1 + 2 * CAP, TILE, COLS)


def all_kernel(table, a_ref, acc_ref, every, inv_ref, held_ref, *refs):
    seeds, new_ref = refs[:-1], refs[-1]
    unroll = 4

    def step(g, c):
        for u in range(unroll):
            t = g * unroll + u
            new_ref[t] = new_labels(table, a_ref, every, acc_ref, inv_ref, held_ref, seeds, t, COLS)
        return c

    lax.fori_loop(0, TILES // unroll, step, 0)
    new_ref[ZERO] = jnp.zeros((TILE, COLS), jnp.bfloat16)


def all_tiles(table, a, acc, every, inv, held, seeds):
    flops = 2 * TILES * (SLOTS - EARLY) * TILE * TILE * COLS
    return pl.pallas_call(
        all_kernel,
        out_shape=in_vmem(POOL, jnp.bfloat16),
        in_specs=[SMEM] + [VMEM] * (5 + len(seeds)),
        out_specs=VMEM,
        compiler_params=pltpu.CompilerParams(vmem_limit_bytes=8 * MIB),
        cost_estimate=pl.CostEstimate(flops=flops, bytes_accessed=16 * MIB, transcendentals=0),
        name="all_tiles",
    )(table, a, acc, every, inv, held, *seeds)


def last_kernel(table, a_ref, acc_in, direct_ref, swapped_ref, inv_ref, held_ref, *refs):
    labels, seeds, (acc_ref, out_ref, every) = refs[:-5], refs[-5:-3], refs[-3:]
    gather_pool(every, labels, direct_ref, swapped_ref)
    add_rest(table, a_ref, every, acc_ref)
    unroll = 4

    def step(g, c):
        for u in range(unroll):
            t = g * unroll + u
            out_ref[t] = new_labels(table, a_ref, every, acc_ref, inv_ref, held_ref, seeds, t, TILE)
        return c

    lax.fori_loop(0, TILES // unroll, step, 0)


def last_tiles(table, a, acc, direct, swapped, inv, held, labels, seeds):
    return pl.pallas_call(
        last_kernel,
        out_shape=(
            in_vmem((TILES, TILE, COLS), jnp.float32),
            jax.ShapeDtypeStruct((TILES, TILE, TILE), jnp.bfloat16),
        ),
        in_specs=[SMEM] + [VMEM] * (6 + len(labels) + len(seeds)),
        out_specs=(VMEM,) * 2,
        input_output_aliases={2: 0},
        scratch_shapes=[pltpu.VMEM(EVERY, jnp.bfloat16)],
        compiler_params=pltpu.CompilerParams(vmem_limit_bytes=8 * MIB),
        name="last_tiles",
    )(table, a, acc, direct, swapped, inv, held, *labels, *seeds)[1]


def shifted(block, step):
    parts, cores = lax.axis_size("dom"), lax.axis_size("col")
    route = []
    for i in range(parts):
        for core, to in ((0, i + step), (1, i - step)):
            if 0 <= to < parts:
                route.append((i * cores + core, to * cores + core))
    return lax.ppermute(block, ("dom", "col"), route)


def swapped_cores(block):
    return lax.ppermute(block, "col", [(0, 1), (1, 0)])


def per_device(seed_data, dataset_order, affinity, neighbour_tiles, clamp_mask):
    part_count = lax.axis_size("dom")
    cell_count, slab = seed_data.shape
    pieces = seed_data.reshape(part_count, cell_count // part_count, slab)
    own = lax.all_to_all(pieces, "dom", split_axis=0, concat_axis=0, tiled=True).reshape(cell_count, slab)
    core = lax.axis_index("col").astype(jnp.int32).reshape(1)
    table, need = tables(neighbour_tiles.reshape(-1), core)
    asked = shifted(need, 1)
    inv, held = stage(affinity, clamp_mask.reshape(TILES, TILE))
    affinity = affinity.reshape(TILES * SLOTS, TILE, TILE)
    half, a = order_rows(dataset_order.reshape(-1), own, affinity)
    labels = (half, swapped_cores(half))
    seeds = labels
    send = pack(asked, labels)
    for iteration in range(ITERS):
        direct = shifted(send, -1)
        if iteration > 0:
            labels = (all_tiles(table, a, acc, every, inv, held, seeds),)
        acc = early(table, a, labels)
        swapped = swapped_cores(direct)
        if iteration == ITERS - 1:
            result = last_tiles(table, a, acc, direct, swapped, inv, held, labels, seeds)
            return result.reshape(cell_count, slab)
        acc, every, send = asked_tiles(table, asked, a, acc, direct, swapped, inv, held, labels, seeds)


def solution(mesh):
    return jax.shard_map(
        per_device,
        mesh=mesh,
        in_specs=(
            P("dom", "col"),
            P("dom", None),
            P("dom", None, None, None),
            P("dom", None),
            P("dom"),
        ),
        out_specs=P("dom", "col"),
        check_vma=False,
    )
```

time: 152 us -> 155 us (1.020)
  the two profiles are of different devices: /device:TPU:30 before, /device:TPU:33 now
where the time goes in v2:
time: 155 us
  Pallas kernels  56.8 us (37%)
  blocking collectives  43.7 us (28%)
  waiting for transfers between devices  29.5 us (19%)
  starting transfers between devices  14.4 us (9%)
  local copies, waits for them, and re-layouts  10.4 us (7%)
    all_to_all x1, blocking collectives, per_device(): lax.all_to_all(pieces, 'dom', split_axis=0, concat_axis=0, tiled=True)  43.7 us
    ppermute x4, waiting for transfers between devices, shifted(): return lax.ppermute(block, ('dom', 'col'), route)  29.5 us
    pallas_call x3, Pallas kernels, early(): pl.pallas_call(early_kernel, out_shape=in_vmem((TILES, TILE, COLS), jnp.f...  15.6 us
    pallas_call x2, Pallas kernels, all_tiles(): pl.pallas_call(all_kernel, out_shape=in_vmem(POOL, jnp.bfloat16), in_spec...  10.4 us
    unnamed x11, local copies, waits for them, and re-layouts  10.3 us
    ppermute x4, starting transfers between devices, shifted(): return lax.ppermute(block, ('dom', 'col'), route)  8.75 us
    pallas_call x1, Pallas kernels, stage(): pl.pallas_call(stage_kernel, out_shape=(jax.ShapeDtypeStruct((TILE, TILE)...  6.83 us
    pallas_call x1, Pallas kernels, last_tiles(): pl.pallas_call(last_kernel, out_shape=(in_vmem((TILES, TILE, COLS), jnp.f...  6.69 us
  transfers between devices with their start and end apart: 8, of which 4 were waited for; matrix products, arithmetic and copies ran while one was open for 0% of the time, Pallas kernels for 25%

profile of v2, /device:TPU:33, one launch (start us, length us, event | category | flops | bytes accessed | tf_op | source)
XLA Modules:
  0.0 155.0 jit_solution(521775855729213510)
XLA Ops:
  0.0 43.7 %all_to_all.5 = bf16[128,32,128]{2,1,0:T(8,128)(2,1)S(1)} all-to-all(bf16[128,32,128]{2,1,0:T(8,128)(2,1)} %bitcast.11), channel_id=1, replica_groups=mesh['dom'=128,'col'=2] {'dom'}, dimensions={0} | all-to-all | bytes 2097152 | tf_op jit(solution)/shard_map/all_to_all | solution.py:376
  44.4 6.6 %order_rows.1 = (bf16[33,128,128]{2,1,0:T(8,128)(2,1)S(1)}, bf16[512,128,128]{2,1,0:T(8,128)(2,1)S(1)}) custom-call(s32[4096]{0:T(1024)S(1)} %bitcast.8, bf16[4096,128]{1,0:T(8,128)(2,1)S(1)} %bitcast.7, bf16[512,128,128]{2,1,0:T(8,128)(2,1)} %bitcast.10), custom_call_target="tpu_custom_call" | custom-call | tf_op jit(solution)/shard_map/order_rows/pallas_call | solution.py:165
  51.0 5.7 %copy-done = bf16[512,128,128]{2,1,0:T(8,128)(2,1)} copy-done((bf16[512,128,128]{2,1,0:T(8,128)(2,1)}, bf16[512,128,128]{2,1,0:T(8,128)(2,1)S(1)}, u32[]{:S(2)}) %copy-start) | copy-done | bytes 16777240
  56.7 3.3 %collective-permute-start.1 = (bf16[33,128,128]{2,1,0:T(8,128)(2,1)S(1)}, bf16[33,128,128]{2,1,0:T(8,128)(2,1)S(1)}, u32[]{:S(2)}, u32[]{:S(2)}) collective-permute-start(bf16[33,128,128]{2,1,0:T(8,128)(2,1)S(1)} %get-tuple-element.21.refs_0_.refs_2_.refs_1_), channel_id=1, source_target_pairs={{0,1},{1,0},{2,3},{3,2},{4,5},{5,4},{6,7},{7,6},{8,9},{9,8},{10,11... | collective-permute-start | bytes 3244040 | tf_op jit(solution)/shard_map/ppermute | solution.py:369
  60.2 5.9 %tables.1 = (s32[1152]{0:T(1024)S(1)}, s32[128]{0:T(128)S(1)}) custom-call(s32[512]{0:T(512)S(1)} %reshape.24.nt_ref, s32[1]{0:T(128)} %bitcast.core_ref), custom_call_target="tpu_custom_call" | custom-call | bytes 16777216 | tf_op jit(solution)/shard_map/tables/pallas_call | solution.py:86
  66.1 2.6 %collective-permute-start = (s32[128]{0:T(128)S(1)}, s32[128]{0:T(128)S(1)}, u32[]{:S(2)}, u32[]{:S(2)}) collective-permute-start(s32[128]{0:T(128)S(1)} %get-tuple-element.20), channel_id=1, source_target_pairs={{0,2},{2,4},{3,1},{4,6},{5,3},{6,8},{7,5},{8,10},{9,7},{10,12},{11... | collective-permute-start | bytes 1544 | tf_op jit(solution)/shard_map/ppermute | solution.py:365
  68.8 1.7 %collective-permute-done.asked = s32[128]{0:T(128)S(1)} collective-permute-done((s32[128]{0:T(128)S(1)}, s32[128]{0:T(128)S(1)}, u32[]{:S(2)}, u32[]{:S(2)}) %collective-permute-start) | collective-permute-done | bytes 544 | tf_op jit(solution)/shard_map/ppermute | solution.py:365
  71.0 2.3 %collective-permute-start.2 = (bf16[4,128,256]{2,1,0:T(8,128)(2,1)S(1)}, bf16[4,128,256]{2,1,0:T(8,128)(2,1)S(1)}, u32[]{:S(2)}, u32[]{:S(2)}) collective-permute-start(bf16[4,128,256]{2,1,0:T(8,128)(2,1)S(1)} %pack.1), channel_id=1, source_target_pairs={{1,3},{2,0},{3,5},{4,2},{5,7},{6,4},{7,9},{8,6},{9,11},{10,8},{11,... | collective-permute-start | bytes 786440 | tf_op jit(solution)/shard_map/ppermute | solution.py:365
  73.3 9.0 %collective-permute-done.2.direct_ref = bf16[4,128,256]{2,1,0:T(8,128)(2,1)S(1)} collective-permute-done((bf16[4,128,256]{2,1,0:T(8,128)(2,1)S(1)}, bf16[4,128,256]{2,1,0:T(8,128)(2,1)S(1)}, u32[]{:S(2)}, u32[]{:S(2)}) %collective-permute-start.2) | collective-permute-done | bytes 262176 | tf_op jit(solution)/shard_map/ppermute | solution.py:365
  82.4 2.3 %collective-permute-start.3 = (bf16[4,128,256]{2,1,0:T(8,128)(2,1)S(1)}, bf16[4,128,256]{2,1,0:T(8,128)(2,1)S(1)}, u32[]{:S(2)}, u32[]{:S(2)}) collective-permute-start(bf16[4,128,256]{2,1,0:T(8,128)(2,1)S(1)} %collective-permute-done.2.direct_ref), channel_id=1, source_target_pairs={{0,1},{1,0},{2,3},{3,2},{4,5},{5,4},{6,7},{7,6},{8,9},{9,8},{10,11... | collective-permute-start | bytes 786440 | tf_op jit(solution)/shard_map/ppermute | solution.py:369
  84.7 6.8 %stage.1 = (f32[128,128]{1,0:T(8,128)S(1)}, f32[128,128]{1,0:T(8,128)S(1)}) custom-call(bf16[32,16,128,128]{3,2,1,0:T(8,128)(2,1)} %a_ref.1, s32[32,128]{1,0:T(8,128)S(1)} %bitcast.9), custom_call_target="tpu_custom_call" | custom-call | flops 8388608 | bytes 16777216 | tf_op jit(solution)/shard_map/stage/pallas_call | solution.py:126
  91.5 3.8 %copy-done.1 = bf16[512,128,128]{2,1,0:T(8,128)(2,1)S(1)} copy-done((bf16[512,128,128]{2,1,0:T(8,128)(2,1)S(1)}, bf16[512,128,128]{2,1,0:T(8,128)(2,1)}, u32[]{:S(2)}) %copy-start.1) | copy-done | bytes 16777240
  95.3 5.1 %early.3.acc_in = f32[32,128,256]{2,1,0:T(8,128)S(1)} custom-call(s32[1152]{0:T(1024)S(1)} %get-tuple-element.18.table, bf16[512,128,128]{2,1,0:T(8,128)(2,1)S(1)} %copy-done.1, bf16[33,128,128]{2,1,0:T(8,128)(2,1)S(1)} %get-tuple-element.21.refs_0_.refs_2_.refs_1_, bf16[33,128,128]{2,1,0:T(8,128)(2,1)S(1)} %collective-permute-done.1.refs_1_.refs_3_.refs_2_), custom_call_target="tpu_custom_call" | custom-call | flops 2684354560 | bytes 16777216 | tf_op jit(solution)/shard_map/early/pallas_call | solution.py:218
  100.4 2.2 %asked_tiles.2 = (f32[32,128,256]{2,1,0:T(8,128)S(1)}, bf16[41,128,256]{2,1,0:T(8,128)(2,1)S(1)}, bf16[4,128,256]{2,1,0:T(8,128)(2,1)S(1)}) custom-call(s32[1152]{0:T(1024)S(1)} %get-tuple-element.18.table, s32[128]{0:T(128)S(1)} %collective-permute-done.asked, bf16[512,128,128]{2,1,0:T(8,128)(2,1)S(1)} %copy-done.1, ...), custom_call_target="tpu_custom_call", output_to_operand_aliasing={{0}: (3, {})} | custom-call | tf_op jit(solution)/shard_map/asked_tiles/pallas_call | solution.py:282
  102.7 1.9 %collective-permute-start.4 = (bf16[4,128,256]{2,1,0:T(8,128)(2,1)S(1)}, bf16[4,128,256]{2,1,0:T(8,128)(2,1)S(1)}, u32[]{:S(2)}, u32[]{:S(2)}) collective-permute-start(bf16[4,128,256]{2,1,0:T(8,128)(2,1)S(1)} %get-tuple-element.26), channel_id=1, source_target_pairs={{1,3},{2,0},{3,5},{4,2},{5,7},{6,4},{7,9},{8,6},{9,11},{10,8},{11,... | collective-permute-start | bytes 786440 | tf_op jit(solution)/shard_map/ppermute | solution.py:365
  104.6 9.4 %collective-permute-done.4.direct_ref = bf16[4,128,256]{2,1,0:T(8,128)(2,1)S(1)} collective-permute-done((bf16[4,128,256]{2,1,0:T(8,128)(2,1)S(1)}, bf16[4,128,256]{2,1,0:T(8,128)(2,1)S(1)}, u32[]{:S(2)}, u32[]{:S(2)}) %collective-permute-start.4) | collective-permute-done | bytes 262176 | tf_op jit(solution)/shard_map/ppermute | solution.py:365
  114.0 5.2 %all_tiles.2.refs_0_ = bf16[33,128,256]{2,1,0:T(8,128)(2,1)S(1)} custom-call(s32[1152]{0:T(1024)S(1)} %get-tuple-element.18.table, bf16[512,128,128]{2,1,0:T(8,128)(2,1)S(1)} %copy-done.1, f32[32,128,256]{2,1,0:T(8,128)S(1)} %get-tuple-element.24.acc_ref, bf16[41,128,256]{2,1,0:T(8,128)(2,1)S(1)} %get-tuple-element.25.every, ...), custom_call_target="tpu_custom_call" | custom-call | flops 1610612736 | bytes 16777216 | tf_op jit(solution)/shard_map/all_tiles/pallas_call | solution.py:316
  119.2 5.2 %early.4.acc_in = f32[32,128,256]{2,1,0:T(8,128)S(1)} custom-call(s32[1152]{0:T(1024)S(1)} %get-tuple-element.18.table, bf16[512,128,128]{2,1,0:T(8,128)(2,1)S(1)} %copy-done.1, bf16[33,128,256]{2,1,0:T(8,128)(2,1)S(1)} %all_tiles.2.refs_0_), custom_call_target="tpu_custom_call" | custom-call | flops 2684354560 | bytes 16777216 | tf_op jit(solution)/shard_map/early/pallas_call | solution.py:218
  124.5 2.0 %asked_tiles.3 = (f32[32,128,256]{2,1,0:T(8,128)S(1)}, bf16[41,128,256]{2,1,0:T(8,128)(2,1)S(1)}, bf16[4,128,256]{2,1,0:T(8,128)(2,1)S(1)}) custom-call(s32[1152]{0:T(1024)S(1)} %get-tuple-element.18.table, s32[128]{0:T(128)S(1)} %collective-permute-done.asked, bf16[512,128,128]{2,1,0:T(8,128)(2,1)S(1)} %copy-done.1, ...), custom_call_target="tpu_custom_call", output_to_operand_aliasing={{0}: (3, {})} | custom-call | tf_op jit(solution)/shard_map/asked_tiles/pallas_call | solution.py:282
  126.4 1.9 %collective-permute-start.6 = (bf16[4,128,256]{2,1,0:T(8,128)(2,1)S(1)}, bf16[4,128,256]{2,1,0:T(8,128)(2,1)S(1)}, u32[]{:S(2)}, u32[]{:S(2)}) collective-permute-start(bf16[4,128,256]{2,1,0:T(8,128)(2,1)S(1)} %get-tuple-element.29), channel_id=1, source_target_pairs={{1,3},{2,0},{3,5},{4,2},{5,7},{6,4},{7,9},{8,6},{9,11},{10,8},{11,... | collective-permute-start | bytes 786440 | tf_op jit(solution)/shard_map/ppermute | solution.py:365
  128.4 9.4 %collective-permute-done.6.direct_ref = bf16[4,128,256]{2,1,0:T(8,128)(2,1)S(1)} collective-permute-done((bf16[4,128,256]{2,1,0:T(8,128)(2,1)S(1)}, bf16[4,128,256]{2,1,0:T(8,128)(2,1)S(1)}, u32[]{:S(2)}, u32[]{:S(2)}) %collective-permute-start.6) | collective-permute-done | bytes 262176 | tf_op jit(solution)/shard_map/ppermute | solution.py:365
  137.8 5.2 %all_tiles.3.refs_0_ = bf16[33,128,256]{2,1,0:T(8,128)(2,1)S(1)} custom-call(s32[1152]{0:T(1024)S(1)} %get-tuple-element.18.table, bf16[512,128,128]{2,1,0:T(8,128)(2,1)S(1)} %copy-done.1, f32[32,128,256]{2,1,0:T(8,128)S(1)} %get-tuple-element.27.acc_ref, bf16[41,128,256]{2,1,0:T(8,128)(2,1)S(1)} %get-tuple-element.28.every, ...), custom_call_target="tpu_custom_call" | custom-call | flops 1610612736 | bytes 16777216 | tf_op jit(solution)/shard_map/all_tiles/pallas_call | solution.py:316
  143.0 5.2 %early.5.acc_in = f32[32,128,256]{2,1,0:T(8,128)S(1)} custom-call(s32[1152]{0:T(1024)S(1)} %get-tuple-element.18.table, bf16[512,128,128]{2,1,0:T(8,128)(2,1)S(1)} %copy-done.1, bf16[33,128,256]{2,1,0:T(8,128)(2,1)S(1)} %all_tiles.3.refs_0_), custom_call_target="tpu_custom_call" | custom-call | flops 2684354560 | bytes 16777216 | tf_op jit(solution)/shard_map/early/pallas_call | solution.py:218
  148.3 6.7 %last_tiles.1 = (f32[32,128,256]{2,1,0:T(8,128)S(1)}, bf16[32,128,128]{2,1,0:T(8,128)(2,1)}) custom-call(s32[1152]{0:T(1024)S(1)} %get-tuple-element.18.table, bf16[512,128,128]{2,1,0:T(8,128)(2,1)S(1)} %copy-done.1, f32[32,128,256]{2,1,0:T(8,128)S(1)} %early.5.acc_in, ...), custom_call_target="tpu_custom_call", output_to_operand_aliasing={{0}: (2, {})} | custom-call | tf_op jit(solution)/shard_map/last_tiles/pallas_call | solution.py:343
  (17 shorter events, 1.5 us)
Async XLA Ops:
  43.7 0.7 copy-start.2
  44.4 15.7 %copy-start.4 = (s32[32,16]{0,1:T(8,128)S(1)}, s32[32,16]{0,1:T(8,128)}, u32[]{:S(2)}) copy-start(s32[32,16]{0,1:T(8,128)} %param.8) | copy-start | bytes 6148
  44.4 40.3 %copy-start.3 = (s32[4096]{0:T(1024)S(1)}, s32[4096]{0:T(1024)}, u32[]{:S(2)}) copy-start(s32[4096]{0:T(1024)} %param.9) | copy-start | bytes 49156
  51.0 5.7 %copy-start = (bf16[512,128,128]{2,1,0:T(8,128)(2,1)}, bf16[512,128,128]{2,1,0:T(8,128)(2,1)S(1)}, u32[]{:S(2)}) copy-start(bf16[512,128,128]{2,1,0:T(8,128)(2,1)S(1)} %get-tuple-element.19.a_ref) | copy-start | bytes 50331652
  56.7 13.7 %collective-permute-start.1 = (bf16[33,128,128]{2,1,0:T(8,128)(2,1)S(1)}, bf16[33,128,128]{2,1,0:T(8,128)(2,1)S(1)}, u32[]{:S(2)}, u32[]{:S(2)}) collective-permute-start(bf16[33,128,128]{2,1,0:T(8,128)(2,1)S(1)} %get-tuple-element.21.refs_0_.refs_2_.refs_1_), channel_id=1, source_target_pairs={{0,1},{1,0},{2,3},{3,2},{4,5},{5,4},{6,7},{7,6},{8,9},{9,8},{10,11... | collective-permute-start | bytes 3244040 | tf_op jit(solution)/shard_map/ppermute | solution.py:369
  66.1 4.3 %collective-permute-start = (s32[128]{0:T(128)S(1)}, s32[128]{0:T(128)S(1)}, u32[]{:S(2)}, u32[]{:S(2)}) collective-permute-start(s32[128]{0:T(128)S(1)} %get-tuple-element.20), channel_id=1, source_target_pairs={{0,2},{2,4},{3,1},{4,6},{5,3},{6,8},{7,5},{8,10},{9,7},{10,12},{11... | collective-permute-start | bytes 1544 | tf_op jit(solution)/shard_map/ppermute | solution.py:365
  71.0 11.3 %collective-permute-start.2 = (bf16[4,128,256]{2,1,0:T(8,128)(2,1)S(1)}, bf16[4,128,256]{2,1,0:T(8,128)(2,1)S(1)}, u32[]{:S(2)}, u32[]{:S(2)}) collective-permute-start(bf16[4,128,256]{2,1,0:T(8,128)(2,1)S(1)} %pack.1), channel_id=1, source_target_pairs={{1,3},{2,0},{3,5},{4,2},{5,7},{6,4},{7,9},{8,6},{9,11},{10,8},{11,... | collective-permute-start | bytes 786440 | tf_op jit(solution)/shard_map/ppermute | solution.py:365
  82.4 18.1 %collective-permute-start.3 = (bf16[4,128,256]{2,1,0:T(8,128)(2,1)S(1)}, bf16[4,128,256]{2,1,0:T(8,128)(2,1)S(1)}, u32[]{:S(2)}, u32[]{:S(2)}) collective-permute-start(bf16[4,128,256]{2,1,0:T(8,128)(2,1)S(1)} %collective-permute-done.2.direct_ref), channel_id=1, source_target_pairs={{0,1},{1,0},{2,3},{3,2},{4,5},{5,4},{6,7},{7,6},{8,9},{9,8},{10,11... | collective-permute-start | bytes 786440 | tf_op jit(solution)/shard_map/ppermute | solution.py:369
  84.7 10.6 %copy-start.1 = (bf16[512,128,128]{2,1,0:T(8,128)(2,1)S(1)}, bf16[512,128,128]{2,1,0:T(8,128)(2,1)}, u32[]{:S(2)}) copy-start(bf16[512,128,128]{2,1,0:T(8,128)(2,1)} %copy-done) | copy-start | bytes 50331652
  102.7 11.3 %collective-permute-start.4 = (bf16[4,128,256]{2,1,0:T(8,128)(2,1)S(1)}, bf16[4,128,256]{2,1,0:T(8,128)(2,1)S(1)}, u32[]{:S(2)}, u32[]{:S(2)}) collective-permute-start(bf16[4,128,256]{2,1,0:T(8,128)(2,1)S(1)} %get-tuple-element.26), channel_id=1, source_target_pairs={{1,3},{2,0},{3,5},{4,2},{5,7},{6,4},{7,9},{8,6},{9,11},{10,8},{11,... | collective-permute-start | bytes 786440 | tf_op jit(solution)/shard_map/ppermute | solution.py:365
  114.0 10.5 %collective-permute-start.5 = (bf16[4,128,256]{2,1,0:T(8,128)(2,1)S(1)}, bf16[4,128,256]{2,1,0:T(8,128)(2,1)S(1)}, u32[]{:S(2)}, u32[]{:S(2)}) collective-permute-start(bf16[4,128,256]{2,1,0:T(8,128)(2,1)S(1)} %collective-permute-done.4.direct_ref), channel_id=1, source_target_pairs={{0,1},{1,0},{2,3},{3,2},{4,5},{5,4},{6,7},{7,6},{8,9},{9,8},{10,11... | collective-permute-start | bytes 786440 | tf_op jit(solution)/shard_map/ppermute | solution.py:369
  126.4 11.3 %collective-permute-start.6 = (bf16[4,128,256]{2,1,0:T(8,128)(2,1)S(1)}, bf16[4,128,256]{2,1,0:T(8,128)(2,1)S(1)}, u32[]{:S(2)}, u32[]{:S(2)}) collective-permute-start(bf16[4,128,256]{2,1,0:T(8,128)(2,1)S(1)} %get-tuple-element.29), channel_id=1, source_target_pairs={{1,3},{2,0},{3,5},{4,2},{5,7},{6,4},{7,9},{8,6},{9,11},{10,8},{11,... | collective-permute-start | bytes 786440 | tf_op jit(solution)/shard_map/ppermute | solution.py:365
  137.8 10.5 %collective-permute-start.7 = (bf16[4,128,256]{2,1,0:T(8,128)(2,1)S(1)}, bf16[4,128,256]{2,1,0:T(8,128)(2,1)S(1)}, u32[]{:S(2)}, u32[]{:S(2)}) collective-permute-start(bf16[4,128,256]{2,1,0:T(8,128)(2,1)S(1)} %collective-permute-done.6.direct_ref), channel_id=1, source_target_pairs={{0,1},{1,0},{2,3},{3,2},{4,5},{5,4},{6,7},{7,6},{8,9},{9,8},{10,11... | collective-permute-start | bytes 786440 | tf_op jit(solution)/shard_map/ppermute | solution.py:369

commit v3 on v2

--- a/solution.py
+++ b/solution.py
@@ -1,3 +1,5 @@
+import functools
+
 import jax
 import jax.numpy as jnp
 from jax import lax
@@ -138,14 +140,11 @@
     )(affinity, clamp)
 
 
-POOL = (TILES + 1, TILE, COLS)
 HALF = (TILES + 1, TILE, TILE)
 SEND = (CAP, TILE, COLS)
 
 
-def order_kernel(order_ref, own_ref, a_ref, half_ref, v_ref, src, dst, sem):
-    load = pltpu.make_async_copy(a_ref, v_ref, sem)
-    load.start()
+def order_kernel(order_ref, own_ref, half_ref, src, dst):
     src[...] = own_ref[...].astype(jnp.float32)
     unroll = 64
 
@@ -158,19 +157,19 @@
     lax.fori_loop(0, TILES * TILE // unroll, step, 0)
     half_ref[0:TILES] = dst[...].astype(jnp.bfloat16).reshape(TILES, TILE, TILE)
     half_ref[ZERO] = jnp.zeros((TILE, TILE), jnp.bfloat16)
-    load.wait()
-
-
-def order_rows(order, own, affinity):
+
+
+def order_rows(order, own):
     return pl.pallas_call(
         order_kernel,
-        out_shape=(in_vmem(HALF, jnp.bfloat16), in_vmem(affinity.shape, jnp.bfloat16)),
-        in_specs=[SMEM, VMEM, pl.BlockSpec(memory_space=pltpu.HBM)],
-        out_specs=(VMEM,) * 2,
-        scratch_shapes=[pltpu.VMEM((TILES * TILE, TILE), jnp.float32)] * 2 + [pltpu.SemaphoreType.DMA],
-        compiler_params=pltpu.CompilerParams(vmem_limit_bytes=32 * MIB),
+        out_shape=in_vmem(HALF, jnp.bfloat16),
+        in_specs=[SMEM, VMEM],
+        out_specs=VMEM,
+        scratch_shapes=[pltpu.VMEM((TILES * TILE, TILE), jnp.float32)] * 2,
+        compiler_params=pltpu.CompilerParams(vmem_limit_bytes=8 * MIB),
+        cost_estimate=pl.CostEstimate(flops=0, bytes_accessed=32 * MIB, transcendentals=0),
         name="order_rows",
-    )(order, own, affinity)
+    )(order, own)
 
 
 def labels_of(refs, tile):
@@ -194,16 +193,29 @@
     )(asked, *labels)
 
 
-def early_kernel(table, a_ref, *refs):
-    acc_ref, labels = refs[-1], refs[:-1]
+def early_kernel(load, table, a_ref, *refs):
     unroll = 4
+    if load:
+        labels, (acc_ref, v_ref, sem) = refs[:-3], refs[-3:]
+    else:
+        labels, acc_ref, v_ref = refs[:-1], refs[-1], a_ref
+
+    def copy(g):
+        part = pl.ds(g * unroll * SLOTS, unroll * SLOTS)
+        return pltpu.make_async_copy(a_ref.at[part], v_ref.at[part], sem.at[g])
+
+    if load:
+        for g in range(TILES // unroll):
+            copy(g).start()
 
     def step(g, c):
+        if load:
+            copy(g).wait()
         for u in range(unroll):
             t = g * unroll + u
             lhs, rhs = [], []
             for k in range(EARLY):
-                lhs.append(a_ref[table[SLOT_AT + t * SLOTS + k]])
+                lhs.append(v_ref[table[SLOT_AT + t * SLOTS + k]])
                 rhs.append(labels_of(labels, jnp.minimum(table[t * SLOTS + k], ZERO)))
             acc_ref[t] = jnp.dot(
                 jnp.concatenate(lhs, axis=1), jnp.concatenate(rhs, axis=0), preferred_element_type=jnp.float32
@@ -213,23 +225,25 @@
     lax.fori_loop(0, TILES // unroll, step, 0)
 
 
-def early(table, a, labels):
+def early(table, a, labels, load=False):
     flops = 2 * TILES * EARLY * TILE * TILE * COLS
-    return pl.pallas_call(
-        early_kernel,
-        out_shape=in_vmem((TILES, TILE, COLS), jnp.float32),
-        in_specs=[SMEM] + [VMEM] * (1 + len(labels)),
-        out_specs=VMEM,
-        compiler_params=pltpu.CompilerParams(vmem_limit_bytes=8 * MIB),
+    acc = in_vmem((TILES, TILE, COLS), jnp.float32)
+    return pl.pallas_call(
+        functools.partial(early_kernel, load),
+        out_shape=(acc, in_vmem(a.shape, a.dtype)) if load else acc,
+        in_specs=[SMEM, pl.BlockSpec(memory_space=pltpu.HBM) if load else VMEM] + [VMEM] * len(labels),
+        out_specs=(VMEM, VMEM) if load else VMEM,
+        scratch_shapes=[pltpu.SemaphoreType.DMA((TILES // 4,))] if load else [],
+        compiler_params=pltpu.CompilerParams(vmem_limit_bytes=(28 if load else 8) * MIB),
         cost_estimate=pl.CostEstimate(flops=flops, bytes_accessed=16 * MIB, transcendentals=0),
-        name="early",
+        name="early_load" if load else "early",
     )(table, a, *labels)
 
 
 def gather_pool(every, labels, direct_ref, swapped_ref):
-    width = COLS // len(labels)
-    for p, ref in enumerate(labels):
-        every[0 : TILES + 1, :, p * width : (p + 1) * width] = ref[...]
+    if len(labels) > 1:
+        for p, ref in enumerate(labels):
+            every[0 : TILES + 1, :, p * TILE : (p + 1) * TILE] = ref[...]
     every[TILES + 1 : TILES + 1 + CAP] = direct_ref[...]
     every[TILES + 1 + CAP :, :, :TILE] = swapped_ref[:, :, TILE:]
     every[TILES + 1 + CAP :, :, TILE:] = swapped_ref[:, :, :TILE]
@@ -288,7 +302,7 @@
         ),
         in_specs=[SMEM] * 2 + [VMEM] * (6 + len(labels) + len(seeds)),
         out_specs=(VMEM,) * 3,
-        input_output_aliases={3: 0},
+        input_output_aliases={3: 0, 8: 1} if len(labels) == 1 else {3: 0},
         compiler_params=pltpu.CompilerParams(vmem_limit_bytes=4 * MIB),
         name="asked_tiles",
     )(table, asked, a, acc, direct, swapped, inv, held, *labels, *seeds)
@@ -315,7 +329,7 @@
     flops = 2 * TILES * (SLOTS - EARLY) * TILE * TILE * COLS
     return pl.pallas_call(
         all_kernel,
-        out_shape=in_vmem(POOL, jnp.bfloat16),
+        out_shape=in_vmem(EVERY, jnp.bfloat16),
         in_specs=[SMEM] + [VMEM] * (5 + len(seeds)),
         out_specs=VMEM,
         compiler_params=pltpu.CompilerParams(vmem_limit_bytes=8 * MIB),
@@ -325,7 +339,7 @@
 
 
 def last_kernel(table, a_ref, acc_in, direct_ref, swapped_ref, inv_ref, held_ref, *refs):
-    labels, seeds, (acc_ref, out_ref, every) = refs[:-5], refs[-5:-3], refs[-3:]
+    labels, seeds, (acc_ref, every, out_ref) = refs[:-5], refs[-5:-3], refs[-3:]
     gather_pool(every, labels, direct_ref, swapped_ref)
     add_rest(table, a_ref, every, acc_ref)
     unroll = 4
@@ -344,15 +358,15 @@
         last_kernel,
         out_shape=(
             in_vmem((TILES, TILE, COLS), jnp.float32),
+            in_vmem(EVERY, jnp.bfloat16),
             jax.ShapeDtypeStruct((TILES, TILE, TILE), jnp.bfloat16),
         ),
         in_specs=[SMEM] + [VMEM] * (6 + len(labels) + len(seeds)),
-        out_specs=(VMEM,) * 2,
-        input_output_aliases={2: 0},
-        scratch_shapes=[pltpu.VMEM(EVERY, jnp.bfloat16)],
+        out_specs=(VMEM,) * 3,
+        input_output_aliases={2: 0, 7: 1},
         compiler_params=pltpu.CompilerParams(vmem_limit_bytes=8 * MIB),
         name="last_tiles",
-    )(table, a, acc, direct, swapped, inv, held, *labels, *seeds)[1]
+    )(table, a, acc, direct, swapped, inv, held, *labels, *seeds)[2]
 
 
 def shifted(block, step):
@@ -378,8 +392,8 @@
     table, need = tables(neighbour_tiles.reshape(-1), core)
     asked = shifted(need, 1)
     inv, held = stage(affinity, clamp_mask.reshape(TILES, TILE))
-    affinity = affinity.reshape(TILES * SLOTS, TILE, TILE)
-    half, a = order_rows(dataset_order.reshape(-1), own, affinity)
+    a = affinity.reshape(TILES * SLOTS, TILE, TILE)
+    half = order_rows(dataset_order.reshape(-1), own)
     labels = (half, swapped_cores(half))
     seeds = labels
     send = pack(asked, labels)
@@ -387,7 +401,10 @@
         direct = shifted(send, -1)
         if iteration > 0:
             labels = (all_tiles(table, a, acc, every, inv, held, seeds),)
-        acc = early(table, a, labels)
+        if iteration:
+            acc = early(table, a, labels)
+        else:
+            acc, a = early(table, a, labels, load=True)
         swapped = swapped_cores(direct)
         if iteration == ITERS - 1:
             result = last_tiles(table, a, acc, direct, swapped, inv, held, labels, seeds)

time: 155 us -> 144 us (0.929)
  local copies, waits for them, and re-layouts: 10.4 us -> 0.88 us
  Pallas kernels: 56.8 us -> 55.2 us
    unnamed x11 -> x7, local copies, waits for them, and re-layouts: 10.3 us -> 0.8 us
  transfers between devices with their start and end apart: 8 -> 8, of which waited for: 4 -> 4; matrix products, arithmetic and copies ran while one was open for 0% -> 0% of each run, Pallas kernels for 25% -> 27%
where the time goes in v3:
time: 144 us
  Pallas kernels  55.2 us (38%)
  blocking collectives  43.8 us (30%)
  waiting for transfers between devices  29.5 us (20%)
  starting transfers between devices  14.5 us (10%)
    all_to_all x1, blocking collectives, per_device(): lax.all_to_all(pieces, 'dom', split_axis=0, concat_axis=0, tiled=True)  43.8 us
    ppermute x4, waiting for transfers between devices, shifted(): return lax.ppermute(block, ('dom', 'col'), route)  29.5 us
    pallas_call x3, Pallas kernels, early(): pl.pallas_call(functools.partial(early_kernel, load), out_shape=(acc, in_...  16.6 us
    pallas_call x2, Pallas kernels, all_tiles(): pl.pallas_call(all_kernel, out_shape=in_vmem(EVERY, jnp.bfloat16), in_spe...  10.3 us
    ppermute x4, starting transfers between devices, shifted(): return lax.ppermute(block, ('dom', 'col'), route)  8.75 us
    pallas_call x1, Pallas kernels, stage(): pl.pallas_call(stage_kernel, out_shape=(jax.ShapeDtypeStruct((TILE, TILE)...  6.69 us
    pallas_call x1, Pallas kernels, last_tiles(): pl.pallas_call(last_kernel, out_shape=(in_vmem((TILES, TILE, COLS), jnp.f...  6.55 us
    pallas_call x1, Pallas kernels, tables(): pl.pallas_call(tables_kernel, out_shape=(i32(REST_AT + 128), i32(128)), i...  5.88 us
  transfers between devices with their start and end apart: 8, of which 4 were waited for; matrix products, arithmetic and copies ran while one was open for 0% of the time, Pallas kernels for 27%

profile of v3, /device:TPU:33, one launch (start us, length us, event | category | flops | bytes accessed | tf_op | source)
XLA Modules:
  0.0 144.1 jit_solution(8991442605919585961)
XLA Ops:
  0.0 43.8 %all_to_all.5 = bf16[128,32,128]{2,1,0:T(8,128)(2,1)S(1)} all-to-all(bf16[128,32,128]{2,1,0:T(8,128)(2,1)} %bitcast.11), channel_id=1, replica_groups=mesh['dom'=128,'col'=2] {'dom'}, dimensions={0} | all-to-all | bytes 2097152 | tf_op jit(solution)/shard_map/all_to_all | solution.py:390
  43.8 0.7 copy-done
  44.5 4.5 %order_rows.1.refs_0_.refs_2_.refs_1_ = bf16[33,128,128]{2,1,0:T(8,128)(2,1)S(1)} custom-call(s32[4096]{0:T(1024)S(1)} %bitcast.8, bf16[4096,128]{1,0:T(8,128)(2,1)S(1)} %bitcast.7), custom_call_target="tpu_custom_call" | custom-call | bytes 33554432 | tf_op jit(solution)/shard_map/order_rows/pallas_call | solution.py:163
  49.1 3.4 %collective-permute-start = (bf16[33,128,128]{2,1,0:T(8,128)(2,1)S(1)}, bf16[33,128,128]{2,1,0:T(8,128)(2,1)S(1)}, u32[]{:S(2)}, u32[]{:S(2)}) collective-permute-start(bf16[33,128,128]{2,1,0:T(8,128)(2,1)S(1)} %order_rows.1.refs_0_.refs_2_.refs_1_), channel_id=1, source_target_pairs={{0,1},{1,0},{2,3},{3,2},{4,5},{5,4},{6,7},{7,6},{8,9},{9,8},{10,11... | collective-permute-start | bytes 3244040 | tf_op jit(solution)/shard_map/ppermute | solution.py:383
  52.7 5.9 %tables.1 = (s32[1152]{0:T(1024)S(1)}, s32[128]{0:T(128)S(1)}) custom-call(s32[512]{0:T(512)S(1)} %reshape.24.nt_ref, s32[1]{0:T(128)} %bitcast.core_ref), custom_call_target="tpu_custom_call" | custom-call | bytes 16777216 | tf_op jit(solution)/shard_map/tables/pallas_call | solution.py:88
  58.6 2.6 %collective-permute-start.1 = (s32[128]{0:T(128)S(1)}, s32[128]{0:T(128)S(1)}, u32[]{:S(2)}, u32[]{:S(2)}) collective-permute-start(s32[128]{0:T(128)S(1)} %get-tuple-element.20), channel_id=1, source_target_pairs={{0,2},{2,4},{3,1},{4,6},{5,3},{6,8},{7,5},{8,10},{9,7},{10,12},{11... | collective-permute-start | bytes 1544 | tf_op jit(solution)/shard_map/ppermute | solution.py:379
  61.2 1.7 %collective-permute-done.1.asked = s32[128]{0:T(128)S(1)} collective-permute-done((s32[128]{0:T(128)S(1)}, s32[128]{0:T(128)S(1)}, u32[]{:S(2)}, u32[]{:S(2)}) %collective-permute-start.1) | collective-permute-done | bytes 544 | tf_op jit(solution)/shard_map/ppermute | solution.py:379
  62.9 0.6 pack.1
  63.5 2.3 %collective-permute-start.2 = (bf16[4,128,256]{2,1,0:T(8,128)(2,1)S(1)}, bf16[4,128,256]{2,1,0:T(8,128)(2,1)S(1)}, u32[]{:S(2)}, u32[]{:S(2)}) collective-permute-start(bf16[4,128,256]{2,1,0:T(8,128)(2,1)S(1)} %pack.1), channel_id=1, source_target_pairs={{1,3},{2,0},{3,5},{4,2},{5,7},{6,4},{7,9},{8,6},{9,11},{10,8},{11,... | collective-permute-start | bytes 786440 | tf_op jit(solution)/shard_map/ppermute | solution.py:379
  65.8 9.0 %collective-permute-done.2.direct_ref = bf16[4,128,256]{2,1,0:T(8,128)(2,1)S(1)} collective-permute-done((bf16[4,128,256]{2,1,0:T(8,128)(2,1)S(1)}, bf16[4,128,256]{2,1,0:T(8,128)(2,1)S(1)}, u32[]{:S(2)}, u32[]{:S(2)}) %collective-permute-start.2) | collective-permute-done | bytes 262176 | tf_op jit(solution)/shard_map/ppermute | solution.py:379
  74.8 2.3 %collective-permute-start.3 = (bf16[4,128,256]{2,1,0:T(8,128)(2,1)S(1)}, bf16[4,128,256]{2,1,0:T(8,128)(2,1)S(1)}, u32[]{:S(2)}, u32[]{:S(2)}) collective-permute-start(bf16[4,128,256]{2,1,0:T(8,128)(2,1)S(1)} %collective-permute-done.2.direct_ref), channel_id=1, source_target_pairs={{0,1},{1,0},{2,3},{3,2},{4,5},{5,4},{6,7},{7,6},{8,9},{9,8},{10,11... | collective-permute-start | bytes 786440 | tf_op jit(solution)/shard_map/ppermute | solution.py:383
  77.1 6.7 %stage.1 = (f32[128,128]{1,0:T(8,128)S(1)}, f32[128,128]{1,0:T(8,128)S(1)}) custom-call(bf16[32,16,128,128]{3,2,1,0:T(8,128)(2,1)} %a_ref.1, s32[32,128]{1,0:T(8,128)S(1)} %bitcast.9), custom_call_target="tpu_custom_call" | custom-call | flops 8388608 | bytes 16777216 | tf_op jit(solution)/shard_map/stage/pallas_call | solution.py:128
  83.8 7.1 %early_load.1 = (f32[32,128,256]{2,1,0:T(8,128)S(1)}, bf16[512,128,128]{2,1,0:T(8,128)(2,1)S(1)}) custom-call(s32[1152]{0:T(1024)S(1)} %get-tuple-element.18.table, bf16[512,128,128]{2,1,0:T(8,128)(2,1)} %bitcast.10, bf16[33,128,128]{2,1,0:T(8,128)(2,1)S(1)} %order_rows.1.refs_0_.refs_2_.refs_1_, ...), custom_call_target="tpu_custom_call" | custom-call | flops 2684354560 | bytes 16777216 | tf_op jit(solution)/shard_map/early_load/pallas_call | solution.py:231
  91.0 2.2 %asked_tiles.2 = (f32[32,128,256]{2,1,0:T(8,128)S(1)}, bf16[41,128,256]{2,1,0:T(8,128)(2,1)S(1)}, bf16[4,128,256]{2,1,0:T(8,128)(2,1)S(1)}) custom-call(s32[1152]{0:T(1024)S(1)} %get-tuple-element.18.table, s32[128]{0:T(128)S(1)} %collective-permute-done.1.asked, ...), custom_call_target="tpu_custom_call", output_to_operand_aliasing={{0}: (3, {})} | custom-call | tf_op jit(solution)/shard_map/asked_tiles/pallas_call | solution.py:296
  93.2 1.9 %collective-permute-start.4 = (bf16[4,128,256]{2,1,0:T(8,128)(2,1)S(1)}, bf16[4,128,256]{2,1,0:T(8,128)(2,1)S(1)}, u32[]{:S(2)}, u32[]{:S(2)}) collective-permute-start(bf16[4,128,256]{2,1,0:T(8,128)(2,1)S(1)} %get-tuple-element.26), channel_id=1, source_target_pairs={{1,3},{2,0},{3,5},{4,2},{5,7},{6,4},{7,9},{8,6},{9,11},{10,8},{11,... | collective-permute-start | bytes 786440 | tf_op jit(solution)/shard_map/ppermute | solution.py:379
  95.1 9.4 %collective-permute-done.4.direct_ref = bf16[4,128,256]{2,1,0:T(8,128)(2,1)S(1)} collective-permute-done((bf16[4,128,256]{2,1,0:T(8,128)(2,1)S(1)}, bf16[4,128,256]{2,1,0:T(8,128)(2,1)S(1)}, u32[]{:S(2)}, u32[]{:S(2)}) %collective-permute-start.4) | collective-permute-done | bytes 262176 | tf_op jit(solution)/shard_map/ppermute | solution.py:379
  104.5 5.2 %all_tiles.2.refs_0_ = bf16[41,128,256]{2,1,0:T(8,128)(2,1)S(1)} custom-call(s32[1152]{0:T(1024)S(1)} %get-tuple-element.18.table, bf16[512,128,128]{2,1,0:T(8,128)(2,1)S(1)} %get-tuple-element.19.a_ref, f32[32,128,256]{2,1,0:T(8,128)S(1)} %get-tuple-element.24.acc_ref, bf16[41,128,256]{2,1,0:T(8,128)(2,1)S(1)} %get-tuple-element.25.every, ...), custom_call_target="tpu_custom_call" | custom-call | flops 1610612736 | bytes 16777216 | tf_op jit(solution)/shard_map/all_tiles/pallas_call | solution.py:330
  109.7 4.8 %early.2.acc_in = f32[32,128,256]{2,1,0:T(8,128)S(1)} custom-call(s32[1152]{0:T(1024)S(1)} %get-tuple-element.18.table, bf16[512,128,128]{2,1,0:T(8,128)(2,1)S(1)} %get-tuple-element.19.a_ref, bf16[41,128,256]{2,1,0:T(8,128)(2,1)S(1)} %all_tiles.2.refs_0_), custom_call_target="tpu_custom_call" | custom-call | flops 2684354560 | bytes 16777216 | tf_op jit(solution)/shard_map/early/pallas_call | solution.py:231
  114.5 1.8 %asked_tiles.3 = (f32[32,128,256]{2,1,0:T(8,128)S(1)}, bf16[41,128,256]{2,1,0:T(8,128)(2,1)S(1)}, bf16[4,128,256]{2,1,0:T(8,128)(2,1)S(1)}) custom-call(s32[1152]{0:T(1024)S(1)} %get-tuple-element.18.table, s32[128]{0:T(128)S(1)} %collective-permute-done.1.asked, ...), custom_call_target="tpu_custom_call", output_to_operand_aliasing={{0}: (3, {}), {1}: (8, {})} | custom-call | tf_op jit(solution)/shard_map/asked_tiles/pallas_call | solution.py:296
  116.4 1.9 %collective-permute-start.6 = (bf16[4,128,256]{2,1,0:T(8,128)(2,1)S(1)}, bf16[4,128,256]{2,1,0:T(8,128)(2,1)S(1)}, u32[]{:S(2)}, u32[]{:S(2)}) collective-permute-start(bf16[4,128,256]{2,1,0:T(8,128)(2,1)S(1)} %get-tuple-element.29), channel_id=1, source_target_pairs={{1,3},{2,0},{3,5},{4,2},{5,7},{6,4},{7,9},{8,6},{9,11},{10,8},{11,... | collective-permute-start | bytes 786440 | tf_op jit(solution)/shard_map/ppermute | solution.py:379
  118.3 9.4 %collective-permute-done.6.direct_ref = bf16[4,128,256]{2,1,0:T(8,128)(2,1)S(1)} collective-permute-done((bf16[4,128,256]{2,1,0:T(8,128)(2,1)S(1)}, bf16[4,128,256]{2,1,0:T(8,128)(2,1)S(1)}, u32[]{:S(2)}, u32[]{:S(2)}) %collective-permute-start.6) | collective-permute-done | bytes 262176 | tf_op jit(solution)/shard_map/ppermute | solution.py:379
  127.7 5.1 %all_tiles.3.refs_0_ = bf16[41,128,256]{2,1,0:T(8,128)(2,1)S(1)} custom-call(s32[1152]{0:T(1024)S(1)} %get-tuple-element.18.table, bf16[512,128,128]{2,1,0:T(8,128)(2,1)S(1)} %get-tuple-element.19.a_ref, f32[32,128,256]{2,1,0:T(8,128)S(1)} %get-tuple-element.27.acc_ref, bf16[41,128,256]{2,1,0:T(8,128)(2,1)S(1)} %get-tuple-element.28.every, ...), custom_call_target="tpu_custom_call" | custom-call | flops 1610612736 | bytes 16777216 | tf_op jit(solution)/shard_map/all_tiles/pallas_call | solution.py:330
  132.8 4.7 %early.3.acc_in = f32[32,128,256]{2,1,0:T(8,128)S(1)} custom-call(s32[1152]{0:T(1024)S(1)} %get-tuple-element.18.table, bf16[512,128,128]{2,1,0:T(8,128)(2,1)S(1)} %get-tuple-element.19.a_ref, bf16[41,128,256]{2,1,0:T(8,128)(2,1)S(1)} %all_tiles.3.refs_0_), custom_call_target="tpu_custom_call" | custom-call | flops 2684354560 | bytes 16777216 | tf_op jit(solution)/shard_map/early/pallas_call | solution.py:231
  137.5 6.5 %last_tiles.1 = (f32[32,128,256]{2,1,0:T(8,128)S(1)}, bf16[41,128,256]{2,1,0:T(8,128)(2,1)S(1)}, bf16[32,128,128]{2,1,0:T(8,128)(2,1)}) custom-call(s32[1152]{0:T(1024)S(1)} %get-tuple-element.18.table, bf16[512,128,128]{2,1,0:T(8,128)(2,1)S(1)} %get-tuple-element.19.a_ref, ...), custom_call_target="tpu_custom_call", output_to_operand_aliasing={{0}: (2, {}), {1}: (7, {})} | custom-call | tf_op jit(solution)/shard_map/last_tiles/pallas_call | solution.py:357
  (13 shorter events, 0.2 us)
Async XLA Ops:
  0.0 52.5 %copy-start.2 = (s32[32,16]{0,1:T(8,128)S(1)}, s32[32,16]{0,1:T(8,128)}, u32[]{:S(2)}) copy-start(s32[32,16]{0,1:T(8,128)} %param.8) | copy-start | bytes 6148
  0.0 77.1 %copy-start.1 = (s32[4096]{0:T(1024)S(1)}, s32[4096]{0:T(1024)}, u32[]{:S(2)}) copy-start(s32[4096]{0:T(1024)} %param.9) | copy-start | bytes 49156
  43.8 0.7 copy-start
  49.1 13.8 %collective-permute-start = (bf16[33,128,128]{2,1,0:T(8,128)(2,1)S(1)}, bf16[33,128,128]{2,1,0:T(8,128)(2,1)S(1)}, u32[]{:S(2)}, u32[]{:S(2)}) collective-permute-start(bf16[33,128,128]{2,1,0:T(8,128)(2,1)S(1)} %order_rows.1.refs_0_.refs_2_.refs_1_), channel_id=1, source_target_pairs={{0,1},{1,0},{2,3},{3,2},{4,5},{5,4},{6,7},{7,6},{8,9},{9,8},{10,11... | collective-permute-start | bytes 3244040 | tf_op jit(solution)/shard_map/ppermute | solution.py:383
  58.6 4.3 %collective-permute-start.1 = (s32[128]{0:T(128)S(1)}, s32[128]{0:T(128)S(1)}, u32[]{:S(2)}, u32[]{:S(2)}) collective-permute-start(s32[128]{0:T(128)S(1)} %get-tuple-element.20), channel_id=1, source_target_pairs={{0,2},{2,4},{3,1},{4,6},{5,3},{6,8},{7,5},{8,10},{9,7},{10,12},{11... | collective-permute-start | bytes 1544 | tf_op jit(solution)/shard_map/ppermute | solution.py:379
  63.5 11.3 %collective-permute-start.2 = (bf16[4,128,256]{2,1,0:T(8,128)(2,1)S(1)}, bf16[4,128,256]{2,1,0:T(8,128)(2,1)S(1)}, u32[]{:S(2)}, u32[]{:S(2)}) collective-permute-start(bf16[4,128,256]{2,1,0:T(8,128)(2,1)S(1)} %pack.1), channel_id=1, source_target_pairs={{1,3},{2,0},{3,5},{4,2},{5,7},{6,4},{7,9},{8,6},{9,11},{10,8},{11,... | collective-permute-start | bytes 786440 | tf_op jit(solution)/shard_map/ppermute | solution.py:379
  74.8 16.2 %collective-permute-start.3 = (bf16[4,128,256]{2,1,0:T(8,128)(2,1)S(1)}, bf16[4,128,256]{2,1,0:T(8,128)(2,1)S(1)}, u32[]{:S(2)}, u32[]{:S(2)}) collective-permute-start(bf16[4,128,256]{2,1,0:T(8,128)(2,1)S(1)} %collective-permute-done.2.direct_ref), channel_id=1, source_target_pairs={{0,1},{1,0},{2,3},{3,2},{4,5},{5,4},{6,7},{7,6},{8,9},{9,8},{10,11... | collective-permute-start | bytes 786440 | tf_op jit(solution)/shard_map/ppermute | solution.py:383
  93.2 11.3 %collective-permute-start.4 = (bf16[4,128,256]{2,1,0:T(8,128)(2,1)S(1)}, bf16[4,128,256]{2,1,0:T(8,128)(2,1)S(1)}, u32[]{:S(2)}, u32[]{:S(2)}) collective-permute-start(bf16[4,128,256]{2,1,0:T(8,128)(2,1)S(1)} %get-tuple-element.26), channel_id=1, source_target_pairs={{1,3},{2,0},{3,5},{4,2},{5,7},{6,4},{7,9},{8,6},{9,11},{10,8},{11,... | collective-permute-start | bytes 786440 | tf_op jit(solution)/shard_map/ppermute | solution.py:379
  104.5 10.0 %collective-permute-start.5 = (bf16[4,128,256]{2,1,0:T(8,128)(2,1)S(1)}, bf16[4,128,256]{2,1,0:T(8,128)(2,1)S(1)}, u32[]{:S(2)}, u32[]{:S(2)}) collective-permute-start(bf16[4,128,256]{2,1,0:T(8,128)(2,1)S(1)} %collective-permute-done.4.direct_ref), channel_id=1, source_target_pairs={{0,1},{1,0},{2,3},{3,2},{4,5},{5,4},{6,7},{7,6},{8,9},{9,8},{10,11... | collective-permute-start | bytes 786440 | tf_op jit(solution)/shard_map/ppermute | solution.py:383
  116.4 11.3 %collective-permute-start.6 = (bf16[4,128,256]{2,1,0:T(8,128)(2,1)S(1)}, bf16[4,128,256]{2,1,0:T(8,128)(2,1)S(1)}, u32[]{:S(2)}, u32[]{:S(2)}) collective-permute-start(bf16[4,128,256]{2,1,0:T(8,128)(2,1)S(1)} %get-tuple-element.29), channel_id=1, source_target_pairs={{1,3},{2,0},{3,5},{4,2},{5,7},{6,4},{7,9},{8,6},{9,11},{10,8},{11,... | collective-permute-start | bytes 786440 | tf_op jit(solution)/shard_map/ppermute | solution.py:379
  127.7 9.8 %collective-permute-start.7 = (bf16[4,128,256]{2,1,0:T(8,128)(2,1)S(1)}, bf16[4,128,256]{2,1,0:T(8,128)(2,1)S(1)}, u32[]{:S(2)}, u32[]{:S(2)}) collective-permute-start(bf16[4,128,256]{2,1,0:T(8,128)(2,1)S(1)} %collective-permute-done.6.direct_ref), channel_id=1, source_target_pairs={{0,1},{1,0},{2,3},{3,2},{4,5},{5,4},{6,7},{7,6},{8,9},{9,8},{10,11... | collective-permute-start | bytes 786440 | tf_op jit(solution)/shard_map/ppermute | solution.py:383

commit v4 on v3

--- a/solution.py
+++ b/solution.py
@@ -97,7 +97,7 @@
     )(nt, core)
 
 
-def stage_kernel(a_ref, clamp_ref, inv_ref, held_ref, v_ref, sem):
+def stage_kernel(a_ref, clamp_ref, inv_ref, v_ref, sem):
     step = 4
     copies = [
         pltpu.make_async_copy(a_ref.at[pl.ds(g * step, step)], v_ref.at[pl.ds(g * step, step)], sem.at[g])
@@ -108,7 +108,7 @@
     lane = lax.broadcasted_iota(jnp.int32, (TILE, TILE), 1)
     inv_ref[...] = jnp.zeros((TILE, TILE), jnp.float32)
     clamp = clamp_ref[...].astype(jnp.float32)
-    held_ref[...] = jnp.concatenate([clamp, jnp.zeros((TILE - TILES, TILE), jnp.float32)], axis=0).T
+    held = jnp.concatenate([clamp, jnp.zeros((TILE - TILES, TILE), jnp.float32)], axis=0).T > 0.5
     for g, c in enumerate(copies):
         c.wait()
 
@@ -122,17 +122,15 @@
             return carry
 
         lax.fori_loop(0, step, body, 0)
+    inv_ref[...] = jnp.where(held, -inv_ref[...], inv_ref[...])
 
 
 def stage(affinity, clamp):
     return pl.pallas_call(
         stage_kernel,
-        out_shape=(
-            jax.ShapeDtypeStruct((TILE, TILE), jnp.float32),
-            jax.ShapeDtypeStruct((TILE, TILE), jnp.float32),
-        ),
+        out_shape=jax.ShapeDtypeStruct((TILE, TILE), jnp.float32),
         in_specs=[pl.BlockSpec(memory_space=pltpu.HBM), VMEM],
-        out_specs=(VMEM,) * 2,
+        out_specs=VMEM,
         scratch_shapes=[pltpu.VMEM(affinity.shape, jnp.bfloat16), pltpu.SemaphoreType.DMA((TILES // 4,))],
         compiler_params=pltpu.CompilerParams(vmem_limit_bytes=42 * MIB),
         cost_estimate=pl.CostEstimate(flops=TILES * SLOTS * TILE * TILE, bytes_accessed=16 * MIB, transcendentals=0),
@@ -265,7 +263,7 @@
         lax.fori_loop(0, TILES, row, 0)
 
 
-def new_labels(table, a_ref, every, acc_ref, inv_ref, held_ref, seeds, t, width):
+def new_labels(table, a_ref, every, acc_ref, inv_ref, seeds, t, width):
     lhs, rhs = [], []
     for k in range(EARLY, SLOTS):
         lhs.append(a_ref[table[SLOT_AT + t * SLOTS + k]])
@@ -275,24 +273,23 @@
     )
     mine = lax.broadcasted_iota(jnp.int32, (TILE, TILE), 1) == t
     inv = jnp.sum(jnp.where(mine, inv_ref[...], 0.0), axis=1, keepdims=True)
-    held = jnp.sum(jnp.where(mine, held_ref[...], 0.0), axis=1, keepdims=True)
     seed = jnp.concatenate([ref[t] for ref in seeds], axis=1).astype(jnp.float32)
     mixed = spread * inv + (1.0 - carry_weight) * seed
     square = mixed * mixed
     mean = jnp.sum(square[:, :TILE] + square[:, TILE:], axis=1, keepdims=True) * (1.0 / COLS)
     scaled = mixed[:, :width] * lax.rsqrt(mean + norm_eps)
-    return jnp.where(held > 0.5, seed[:, :width], scaled).astype(jnp.bfloat16)
-
-
-def asked_kernel(table, asked, a_ref, acc_in, direct_ref, swapped_ref, inv_ref, held_ref, *refs):
+    return jnp.where(inv < 0.0, seed[:, :width], scaled).astype(jnp.bfloat16)
+
+
+def asked_kernel(table, asked, a_ref, acc_in, direct_ref, swapped_ref, inv_ref, *refs):
     labels, seeds, (acc_ref, every, send_ref) = refs[:-5], refs[-5:-3], refs[-3:]
     gather_pool(every, labels, direct_ref, swapped_ref)
     add_rest(table, a_ref, every, acc_ref)
     for r in range(CAP):
-        send_ref[r] = new_labels(table, a_ref, every, acc_ref, inv_ref, held_ref, seeds, asked[r], COLS)
-
-
-def asked_tiles(table, asked, a, acc, direct, swapped, inv, held, labels, seeds):
+        send_ref[r] = new_labels(table, a_ref, every, acc_ref, inv_ref, seeds, asked[r], COLS)
+
+
+def asked_tiles(table, asked, a, acc, direct, swapped, inv, labels, seeds):
     return pl.pallas_call(
         asked_kernel,
         out_shape=(
@@ -300,60 +297,60 @@
             in_vmem(EVERY, jnp.bfloat16),
             in_vmem(SEND, jnp.bfloat16),
         ),
-        in_specs=[SMEM] * 2 + [VMEM] * (6 + len(labels) + len(seeds)),
+        in_specs=[SMEM] * 2 + [VMEM] * (5 + len(labels) + len(seeds)),
         out_specs=(VMEM,) * 3,
-        input_output_aliases={3: 0, 8: 1} if len(labels) == 1 else {3: 0},
+        input_output_aliases={3: 0, 7: 1} if len(labels) == 1 else {3: 0},
         compiler_params=pltpu.CompilerParams(vmem_limit_bytes=4 * MIB),
         name="asked_tiles",
-    )(table, asked, a, acc, direct, swapped, inv, held, *labels, *seeds)
+    )(table, asked, a, acc, direct, swapped, inv, *labels, *seeds)
 
 
 EVERY = (TILES + 1 + 2 * CAP, TILE, COLS)
 
 
-def all_kernel(table, a_ref, acc_ref, every, inv_ref, held_ref, *refs):
+def all_kernel(table, a_ref, acc_ref, every, inv_ref, *refs):
     seeds, new_ref = refs[:-1], refs[-1]
-    unroll = 4
+    unroll = 8
 
     def step(g, c):
         for u in range(unroll):
             t = g * unroll + u
-            new_ref[t] = new_labels(table, a_ref, every, acc_ref, inv_ref, held_ref, seeds, t, COLS)
+            new_ref[t] = new_labels(table, a_ref, every, acc_ref, inv_ref, seeds, t, COLS)
         return c
 
     lax.fori_loop(0, TILES // unroll, step, 0)
     new_ref[ZERO] = jnp.zeros((TILE, COLS), jnp.bfloat16)
 
 
-def all_tiles(table, a, acc, every, inv, held, seeds):
+def all_tiles(table, a, acc, every, inv, seeds):
     flops = 2 * TILES * (SLOTS - EARLY) * TILE * TILE * COLS
     return pl.pallas_call(
         all_kernel,
         out_shape=in_vmem(EVERY, jnp.bfloat16),
-        in_specs=[SMEM] + [VMEM] * (5 + len(seeds)),
+        in_specs=[SMEM] + [VMEM] * (4 + len(seeds)),
         out_specs=VMEM,
         compiler_params=pltpu.CompilerParams(vmem_limit_bytes=8 * MIB),
         cost_estimate=pl.CostEstimate(flops=flops, bytes_accessed=16 * MIB, transcendentals=0),
         name="all_tiles",
-    )(table, a, acc, every, inv, held, *seeds)
-
-
-def last_kernel(table, a_ref, acc_in, direct_ref, swapped_ref, inv_ref, held_ref, *refs):
+    )(table, a, acc, every, inv, *seeds)
+
+
+def last_kernel(table, a_ref, acc_in, direct_ref, swapped_ref, inv_ref, *refs):
     labels, seeds, (acc_ref, every, out_ref) = refs[:-5], refs[-5:-3], refs[-3:]
     gather_pool(every, labels, direct_ref, swapped_ref)
     add_rest(table, a_ref, every, acc_ref)
-    unroll = 4
+    unroll = 8
 
     def step(g, c):
         for u in range(unroll):
             t = g * unroll + u
-            out_ref[t] = new_labels(table, a_ref, every, acc_ref, inv_ref, held_ref, seeds, t, TILE)
+            out_ref[t] = new_labels(table, a_ref, every, acc_ref, inv_ref, seeds, t, TILE)
         return c
 
     lax.fori_loop(0, TILES // unroll, step, 0)
 
 
-def last_tiles(table, a, acc, direct, swapped, inv, held, labels, seeds):
+def last_tiles(table, a, acc, direct, swapped, inv, labels, seeds):
     return pl.pallas_call(
         last_kernel,
         out_shape=(
@@ -361,12 +358,12 @@
             in_vmem(EVERY, jnp.bfloat16),
             jax.ShapeDtypeStruct((TILES, TILE, TILE), jnp.bfloat16),
         ),
-        in_specs=[SMEM] + [VMEM] * (6 + len(labels) + len(seeds)),
+        in_specs=[SMEM] + [VMEM] * (5 + len(labels) + len(seeds)),
         out_specs=(VMEM,) * 3,
-        input_output_aliases={2: 0, 7: 1},
+        input_output_aliases={2: 0, 6: 1},
         compiler_params=pltpu.CompilerParams(vmem_limit_bytes=8 * MIB),
         name="last_tiles",
-    )(table, a, acc, direct, swapped, inv, held, *labels, *seeds)[2]
+    )(table, a, acc, direct, swapped, inv, *labels, *seeds)[2]
 
 
 def shifted(block, step):
@@ -391,7 +388,7 @@
     core = lax.axis_index("col").astype(jnp.int32).reshape(1)
     table, need = tables(neighbour_tiles.reshape(-1), core)
     asked = shifted(need, 1)
-    inv, held = stage(affinity, clamp_mask.reshape(TILES, TILE))
+    inv = stage(affinity, clamp_mask.reshape(TILES, TILE))
     a = affinity.reshape(TILES * SLOTS, TILE, TILE)
     half = order_rows(dataset_order.reshape(-1), own)
     labels = (half, swapped_cores(half))
@@ -400,16 +397,16 @@
     for iteration in range(ITERS):
         direct = shifted(send, -1)
         if iteration > 0:
-            labels = (all_tiles(table, a, acc, every, inv, held, seeds),)
+            labels = (all_tiles(table, a, acc, every, inv, seeds),)
         if iteration:
             acc = early(table, a, labels)
         else:
             acc, a = early(table, a, labels, load=True)
         swapped = swapped_cores(direct)
         if iteration == ITERS - 1:
-            result = last_tiles(table, a, acc, direct, swapped, inv, held, labels, seeds)
+            result = last_tiles(table, a, acc, direct, swapped, inv, labels, seeds)
             return result.reshape(cell_count, slab)
-        acc, every, send = asked_tiles(table, asked, a, acc, direct, swapped, inv, held, labels, seeds)
+        acc, every, send = asked_tiles(table, asked, a, acc, direct, swapped, inv, labels, seeds)
 
 
 def solution(mesh):

time: 144 us -> 142 us (0.986)
  Pallas kernels: 55.2 us -> 52.9 us
    pallas_call x2, Pallas kernels: 10.3 us -> 8.64 us  [all_tiles(): pl.pallas_call(all_kernel, out_shape=in_vmem(EVERY, jnp.bfloat16), in_spe...]
where the time goes in v4:
time: 142 us
  Pallas kernels  52.9 us (37%)
  blocking collectives  43.8 us (31%)
  waiting for transfers between devices  29.5 us (21%)
  starting transfers between devices  14.5 us (10%)
    all_to_all x1, blocking collectives, per_device(): lax.all_to_all(pieces, 'dom', split_axis=0, concat_axis=0, tiled=True)  43.8 us
    ppermute x4, waiting for transfers between devices, shifted(): return lax.ppermute(block, ('dom', 'col'), route)  29.5 us
    pallas_call x3, Pallas kernels, early(): pl.pallas_call(functools.partial(early_kernel, load), out_shape=(acc, in_...  16.7 us
    ppermute x4, starting transfers between devices, shifted(): return lax.ppermute(block, ('dom', 'col'), route)  8.75 us
    pallas_call x2, Pallas kernels, all_tiles(): pl.pallas_call(all_kernel, out_shape=in_vmem(EVERY, jnp.bfloat16), in_spe...  8.64 us
    pallas_call x1, Pallas kernels, stage(): pl.pallas_call(stage_kernel, out_shape=jax.ShapeDtypeStruct((TILE, TILE),...  6.73 us
    pallas_call x1, Pallas kernels, tables(): pl.pallas_call(tables_kernel, out_shape=(i32(REST_AT + 128), i32(128)), i...  5.88 us
    pallas_call x1, Pallas kernels, last_tiles(): pl.pallas_call(last_kernel, out_shape=(in_vmem((TILES, TILE, COLS), jnp.f...  5.82 us
  transfers between devices with their start and end apart: 8, of which 4 were waited for; matrix products, arithmetic and copies ran while one was open for 0% of the time, Pallas kernels for 27%

profile of v4, /device:TPU:33, one launch (start us, length us, event | category | flops | bytes accessed | tf_op | source)
XLA Modules:
  0.0 141.8 jit_solution(10857563328976851620)
XLA Ops:
  0.0 43.8 %all_to_all.5 = bf16[128,32,128]{2,1,0:T(8,128)(2,1)S(1)} all-to-all(bf16[128,32,128]{2,1,0:T(8,128)(2,1)} %bitcast.11), channel_id=1, replica_groups=mesh['dom'=128,'col'=2] {'dom'}, dimensions={0} | all-to-all | bytes 2097152 | tf_op jit(solution)/shard_map/all_to_all | solution.py:387
  43.8 0.7 copy-done
  44.5 4.5 %order_rows.1.refs_0_.refs_2_.refs_1_ = bf16[33,128,128]{2,1,0:T(8,128)(2,1)S(1)} custom-call(s32[4096]{0:T(1024)S(1)} %bitcast.8, bf16[4096,128]{1,0:T(8,128)(2,1)S(1)} %bitcast.7), custom_call_target="tpu_custom_call" | custom-call | bytes 33554432 | tf_op jit(solution)/shard_map/order_rows/pallas_call | solution.py:161
  49.1 3.4 %collective-permute-start = (bf16[33,128,128]{2,1,0:T(8,128)(2,1)S(1)}, bf16[33,128,128]{2,1,0:T(8,128)(2,1)S(1)}, u32[]{:S(2)}, u32[]{:S(2)}) collective-permute-start(bf16[33,128,128]{2,1,0:T(8,128)(2,1)S(1)} %order_rows.1.refs_0_.refs_2_.refs_1_), channel_id=1, source_target_pairs={{0,1},{1,0},{2,3},{3,2},{4,5},{5,4},{6,7},{7,6},{8,9},{9,8},{10,11... | collective-permute-start | bytes 3244040 | tf_op jit(solution)/shard_map/ppermute | solution.py:380
  52.7 5.9 %tables.1 = (s32[1152]{0:T(1024)S(1)}, s32[128]{0:T(128)S(1)}) custom-call(s32[512]{0:T(512)S(1)} %reshape.24.nt_ref, s32[1]{0:T(128)} %bitcast.core_ref), custom_call_target="tpu_custom_call" | custom-call | bytes 16777216 | tf_op jit(solution)/shard_map/tables/pallas_call | solution.py:88
  58.6 2.6 %collective-permute-start.1 = (s32[128]{0:T(128)S(1)}, s32[128]{0:T(128)S(1)}, u32[]{:S(2)}, u32[]{:S(2)}) collective-permute-start(s32[128]{0:T(128)S(1)} %get-tuple-element.18), channel_id=1, source_target_pairs={{0,2},{2,4},{3,1},{4,6},{5,3},{6,8},{7,5},{8,10},{9,7},{10,12},{11... | collective-permute-start | bytes 1544 | tf_op jit(solution)/shard_map/ppermute | solution.py:376
  61.2 1.7 %collective-permute-done.1.asked = s32[128]{0:T(128)S(1)} collective-permute-done((s32[128]{0:T(128)S(1)}, s32[128]{0:T(128)S(1)}, u32[]{:S(2)}, u32[]{:S(2)}) %collective-permute-start.1) | collective-permute-done | bytes 544 | tf_op jit(solution)/shard_map/ppermute | solution.py:376
  62.9 0.6 pack.1
  63.5 2.3 %collective-permute-start.2 = (bf16[4,128,256]{2,1,0:T(8,128)(2,1)S(1)}, bf16[4,128,256]{2,1,0:T(8,128)(2,1)S(1)}, u32[]{:S(2)}, u32[]{:S(2)}) collective-permute-start(bf16[4,128,256]{2,1,0:T(8,128)(2,1)S(1)} %pack.1), channel_id=1, source_target_pairs={{1,3},{2,0},{3,5},{4,2},{5,7},{6,4},{7,9},{8,6},{9,11},{10,8},{11,... | collective-permute-start | bytes 786440 | tf_op jit(solution)/shard_map/ppermute | solution.py:376
  65.8 9.0 %collective-permute-done.2.direct_ref = bf16[4,128,256]{2,1,0:T(8,128)(2,1)S(1)} collective-permute-done((bf16[4,128,256]{2,1,0:T(8,128)(2,1)S(1)}, bf16[4,128,256]{2,1,0:T(8,128)(2,1)S(1)}, u32[]{:S(2)}, u32[]{:S(2)}) %collective-permute-start.2) | collective-permute-done | bytes 262176 | tf_op jit(solution)/shard_map/ppermute | solution.py:376
  74.8 2.3 %collective-permute-start.3 = (bf16[4,128,256]{2,1,0:T(8,128)(2,1)S(1)}, bf16[4,128,256]{2,1,0:T(8,128)(2,1)S(1)}, u32[]{:S(2)}, u32[]{:S(2)}) collective-permute-start(bf16[4,128,256]{2,1,0:T(8,128)(2,1)S(1)} %collective-permute-done.2.direct_ref), channel_id=1, source_target_pairs={{0,1},{1,0},{2,3},{3,2},{4,5},{5,4},{6,7},{7,6},{8,9},{9,8},{10,11... | collective-permute-start | bytes 786440 | tf_op jit(solution)/shard_map/ppermute | solution.py:380
  77.1 6.7 %stage.1.inv_ref = f32[128,128]{1,0:T(8,128)S(1)} custom-call(bf16[32,16,128,128]{3,2,1,0:T(8,128)(2,1)} %a_ref.1, s32[32,128]{1,0:T(8,128)S(1)} %bitcast.9), custom_call_target="tpu_custom_call" | custom-call | flops 8388608 | bytes 16777216 | tf_op jit(solution)/shard_map/stage/pallas_call | solution.py:129
  83.9 7.2 %early_load.1 = (f32[32,128,256]{2,1,0:T(8,128)S(1)}, bf16[512,128,128]{2,1,0:T(8,128)(2,1)S(1)}) custom-call(s32[1152]{0:T(1024)S(1)} %get-tuple-element.16.table, bf16[512,128,128]{2,1,0:T(8,128)(2,1)} %bitcast.10, bf16[33,128,128]{2,1,0:T(8,128)(2,1)S(1)} %order_rows.1.refs_0_.refs_2_.refs_1_, ...), custom_call_target="tpu_custom_call" | custom-call | flops 2684354560 | bytes 16777216 | tf_op jit(solution)/shard_map/early_load/pallas_call | solution.py:229
  91.1 2.2 %asked_tiles.2 = (f32[32,128,256]{2,1,0:T(8,128)S(1)}, bf16[41,128,256]{2,1,0:T(8,128)(2,1)S(1)}, bf16[4,128,256]{2,1,0:T(8,128)(2,1)S(1)}) custom-call(s32[1152]{0:T(1024)S(1)} %get-tuple-element.16.table, s32[128]{0:T(128)S(1)} %collective-permute-done.1.asked, ...), custom_call_target="tpu_custom_call", output_to_operand_aliasing={{0}: (3, {})} | custom-call | tf_op jit(solution)/shard_map/asked_tiles/pallas_call | solution.py:293
  93.3 1.9 %collective-permute-start.4 = (bf16[4,128,256]{2,1,0:T(8,128)(2,1)S(1)}, bf16[4,128,256]{2,1,0:T(8,128)(2,1)S(1)}, u32[]{:S(2)}, u32[]{:S(2)}) collective-permute-start(bf16[4,128,256]{2,1,0:T(8,128)(2,1)S(1)} %get-tuple-element.22), channel_id=1, source_target_pairs={{1,3},{2,0},{3,5},{4,2},{5,7},{6,4},{7,9},{8,6},{9,11},{10,8},{11,... | collective-permute-start | bytes 786440 | tf_op jit(solution)/shard_map/ppermute | solution.py:376
  95.2 9.4 %collective-permute-done.4.direct_ref = bf16[4,128,256]{2,1,0:T(8,128)(2,1)S(1)} collective-permute-done((bf16[4,128,256]{2,1,0:T(8,128)(2,1)S(1)}, bf16[4,128,256]{2,1,0:T(8,128)(2,1)S(1)}, u32[]{:S(2)}, u32[]{:S(2)}) %collective-permute-start.4) | collective-permute-done | bytes 262176 | tf_op jit(solution)/shard_map/ppermute | solution.py:376
  104.6 4.4 %all_tiles.2.refs_0_ = bf16[41,128,256]{2,1,0:T(8,128)(2,1)S(1)} custom-call(s32[1152]{0:T(1024)S(1)} %get-tuple-element.16.table, bf16[512,128,128]{2,1,0:T(8,128)(2,1)S(1)} %get-tuple-element.17.a_ref, f32[32,128,256]{2,1,0:T(8,128)S(1)} %get-tuple-element.20.acc_ref, bf16[41,128,256]{2,1,0:T(8,128)(2,1)S(1)} %get-tuple-element.21.every, ...), custom_call_target="tpu_custom_call" | custom-call | flops 1610612736 | bytes 16777216 | tf_op jit(solution)/shard_map/all_tiles/pallas_call | solution.py:327
  109.0 4.8 %early.2.acc_in = f32[32,128,256]{2,1,0:T(8,128)S(1)} custom-call(s32[1152]{0:T(1024)S(1)} %get-tuple-element.16.table, bf16[512,128,128]{2,1,0:T(8,128)(2,1)S(1)} %get-tuple-element.17.a_ref, bf16[41,128,256]{2,1,0:T(8,128)(2,1)S(1)} %all_tiles.2.refs_0_), custom_call_target="tpu_custom_call" | custom-call | flops 2684354560 | bytes 16777216 | tf_op jit(solution)/shard_map/early/pallas_call | solution.py:229
  113.8 1.8 %asked_tiles.3 = (f32[32,128,256]{2,1,0:T(8,128)S(1)}, bf16[41,128,256]{2,1,0:T(8,128)(2,1)S(1)}, bf16[4,128,256]{2,1,0:T(8,128)(2,1)S(1)}) custom-call(s32[1152]{0:T(1024)S(1)} %get-tuple-element.16.table, s32[128]{0:T(128)S(1)} %collective-permute-done.1.asked, ...), custom_call_target="tpu_custom_call", output_to_operand_aliasing={{0}: (3, {}), {1}: (7, {})} | custom-call | tf_op jit(solution)/shard_map/asked_tiles/pallas_call | solution.py:293
  115.6 1.9 %collective-permute-start.6 = (bf16[4,128,256]{2,1,0:T(8,128)(2,1)S(1)}, bf16[4,128,256]{2,1,0:T(8,128)(2,1)S(1)}, u32[]{:S(2)}, u32[]{:S(2)}) collective-permute-start(bf16[4,128,256]{2,1,0:T(8,128)(2,1)S(1)} %get-tuple-element.25), channel_id=1, source_target_pairs={{1,3},{2,0},{3,5},{4,2},{5,7},{6,4},{7,9},{8,6},{9,11},{10,8},{11,... | collective-permute-start | bytes 786440 | tf_op jit(solution)/shard_map/ppermute | solution.py:376
  117.5 9.4 %collective-permute-done.6.direct_ref = bf16[4,128,256]{2,1,0:T(8,128)(2,1)S(1)} collective-permute-done((bf16[4,128,256]{2,1,0:T(8,128)(2,1)S(1)}, bf16[4,128,256]{2,1,0:T(8,128)(2,1)S(1)}, u32[]{:S(2)}, u32[]{:S(2)}) %collective-permute-start.6) | collective-permute-done | bytes 262176 | tf_op jit(solution)/shard_map/ppermute | solution.py:376
  126.9 4.3 %all_tiles.3.refs_0_ = bf16[41,128,256]{2,1,0:T(8,128)(2,1)S(1)} custom-call(s32[1152]{0:T(1024)S(1)} %get-tuple-element.16.table, bf16[512,128,128]{2,1,0:T(8,128)(2,1)S(1)} %get-tuple-element.17.a_ref, f32[32,128,256]{2,1,0:T(8,128)S(1)} %get-tuple-element.23.acc_ref, bf16[41,128,256]{2,1,0:T(8,128)(2,1)S(1)} %get-tuple-element.24.every, ...), custom_call_target="tpu_custom_call" | custom-call | flops 1610612736 | bytes 16777216 | tf_op jit(solution)/shard_map/all_tiles/pallas_call | solution.py:327
  131.2 4.8 %early.3.acc_in = f32[32,128,256]{2,1,0:T(8,128)S(1)} custom-call(s32[1152]{0:T(1024)S(1)} %get-tuple-element.16.table, bf16[512,128,128]{2,1,0:T(8,128)(2,1)S(1)} %get-tuple-element.17.a_ref, bf16[41,128,256]{2,1,0:T(8,128)(2,1)S(1)} %all_tiles.3.refs_0_), custom_call_target="tpu_custom_call" | custom-call | flops 2684354560 | bytes 16777216 | tf_op jit(solution)/shard_map/early/pallas_call | solution.py:229
  136.0 5.8 %last_tiles.1 = (f32[32,128,256]{2,1,0:T(8,128)S(1)}, bf16[41,128,256]{2,1,0:T(8,128)(2,1)S(1)}, bf16[32,128,128]{2,1,0:T(8,128)(2,1)}) custom-call(s32[1152]{0:T(1024)S(1)} %get-tuple-element.16.table, bf16[512,128,128]{2,1,0:T(8,128)(2,1)S(1)} %get-tuple-element.17.a_ref, ...), custom_call_target="tpu_custom_call", output_to_operand_aliasing={{0}: (2, {}), {1}: (6, {})} | custom-call | tf_op jit(solution)/shard_map/last_tiles/pallas_call | solution.py:354
  (13 shorter events, 0.2 us)
Async XLA Ops:
  0.0 52.5 %copy-start.2 = (s32[32,16]{0,1:T(8,128)S(1)}, s32[32,16]{0,1:T(8,128)}, u32[]{:S(2)}) copy-start(s32[32,16]{0,1:T(8,128)} %param.8) | copy-start | bytes 6148
  0.0 77.1 %copy-start.1 = (s32[4096]{0:T(1024)S(1)}, s32[4096]{0:T(1024)}, u32[]{:S(2)}) copy-start(s32[4096]{0:T(1024)} %param.9) | copy-start | bytes 49156
  43.8 0.7 copy-start
  49.1 13.8 %collective-permute-start = (bf16[33,128,128]{2,1,0:T(8,128)(2,1)S(1)}, bf16[33,128,128]{2,1,0:T(8,128)(2,1)S(1)}, u32[]{:S(2)}, u32[]{:S(2)}) collective-permute-start(bf16[33,128,128]{2,1,0:T(8,128)(2,1)S(1)} %order_rows.1.refs_0_.refs_2_.refs_1_), channel_id=1, source_target_pairs={{0,1},{1,0},{2,3},{3,2},{4,5},{5,4},{6,7},{7,6},{8,9},{9,8},{10,11... | collective-permute-start | bytes 3244040 | tf_op jit(solution)/shard_map/ppermute | solution.py:380
  58.6 4.3 %collective-permute-start.1 = (s32[128]{0:T(128)S(1)}, s32[128]{0:T(128)S(1)}, u32[]{:S(2)}, u32[]{:S(2)}) collective-permute-start(s32[128]{0:T(128)S(1)} %get-tuple-element.18), channel_id=1, source_target_pairs={{0,2},{2,4},{3,1},{4,6},{5,3},{6,8},{7,5},{8,10},{9,7},{10,12},{11... | collective-permute-start | bytes 1544 | tf_op jit(solution)/shard_map/ppermute | solution.py:376
  63.5 11.3 %collective-permute-start.2 = (bf16[4,128,256]{2,1,0:T(8,128)(2,1)S(1)}, bf16[4,128,256]{2,1,0:T(8,128)(2,1)S(1)}, u32[]{:S(2)}, u32[]{:S(2)}) collective-permute-start(bf16[4,128,256]{2,1,0:T(8,128)(2,1)S(1)} %pack.1), channel_id=1, source_target_pairs={{1,3},{2,0},{3,5},{4,2},{5,7},{6,4},{7,9},{8,6},{9,11},{10,8},{11,... | collective-permute-start | bytes 786440 | tf_op jit(solution)/shard_map/ppermute | solution.py:376
  74.8 16.2 %collective-permute-start.3 = (bf16[4,128,256]{2,1,0:T(8,128)(2,1)S(1)}, bf16[4,128,256]{2,1,0:T(8,128)(2,1)S(1)}, u32[]{:S(2)}, u32[]{:S(2)}) collective-permute-start(bf16[4,128,256]{2,1,0:T(8,128)(2,1)S(1)} %collective-permute-done.2.direct_ref), channel_id=1, source_target_pairs={{0,1},{1,0},{2,3},{3,2},{4,5},{5,4},{6,7},{7,6},{8,9},{9,8},{10,11... | collective-permute-start | bytes 786440 | tf_op jit(solution)/shard_map/ppermute | solution.py:380
  93.3 11.3 %collective-permute-start.4 = (bf16[4,128,256]{2,1,0:T(8,128)(2,1)S(1)}, bf16[4,128,256]{2,1,0:T(8,128)(2,1)S(1)}, u32[]{:S(2)}, u32[]{:S(2)}) collective-permute-start(bf16[4,128,256]{2,1,0:T(8,128)(2,1)S(1)} %get-tuple-element.22), channel_id=1, source_target_pairs={{1,3},{2,0},{3,5},{4,2},{5,7},{6,4},{7,9},{8,6},{9,11},{10,8},{11,... | collective-permute-start | bytes 786440 | tf_op jit(solution)/shard_map/ppermute | solution.py:376
  104.6 9.1 %collective-permute-start.5 = (bf16[4,128,256]{2,1,0:T(8,128)(2,1)S(1)}, bf16[4,128,256]{2,1,0:T(8,128)(2,1)S(1)}, u32[]{:S(2)}, u32[]{:S(2)}) collective-permute-start(bf16[4,128,256]{2,1,0:T(8,128)(2,1)S(1)} %collective-permute-done.4.direct_ref), channel_id=1, source_target_pairs={{0,1},{1,0},{2,3},{3,2},{4,5},{5,4},{6,7},{7,6},{8,9},{9,8},{10,11... | collective-permute-start | bytes 786440 | tf_op jit(solution)/shard_map/ppermute | solution.py:380
  115.6 11.3 %collective-permute-start.6 = (bf16[4,128,256]{2,1,0:T(8,128)(2,1)S(1)}, bf16[4,128,256]{2,1,0:T(8,128)(2,1)S(1)}, u32[]{:S(2)}, u32[]{:S(2)}) collective-permute-start(bf16[4,128,256]{2,1,0:T(8,128)(2,1)S(1)} %get-tuple-element.25), channel_id=1, source_target_pairs={{1,3},{2,0},{3,5},{4,2},{5,7},{6,4},{7,9},{8,6},{9,11},{10,8},{11,... | collective-permute-start | bytes 786440 | tf_op jit(solution)/shard_map/ppermute | solution.py:376
  126.9 9.1 %collective-permute-start.7 = (bf16[4,128,256]{2,1,0:T(8,128)(2,1)S(1)}, bf16[4,128,256]{2,1,0:T(8,128)(2,1)S(1)}, u32[]{:S(2)}, u32[]{:S(2)}) collective-permute-start(bf16[4,128,256]{2,1,0:T(8,128)(2,1)S(1)} %collective-permute-done.6.direct_ref), channel_id=1, source_target_pairs={{0,1},{1,0},{2,3},{3,2},{4,5},{5,4},{6,7},{7,6},{8,9},{9,8},{10,11... | collective-permute-start | bytes 786440 | tf_op jit(solution)/shard_map/ppermute | solution.py:380
